TPU v7x, 32 devices: a whole 2x2x4 slice. The times are simulated.
32 devices in a mesh: ctx: 16 (over z, y, x), tp: 2 (over core).
Axes of the slice: x: 2, y: 2, z: 4, core: 2. Of those that a mesh axis runs over, the one named last changes fastest.
Arguments:
- ssm_input: bfloat16 [2048, 8192], P('ctx', 'tp'), may hold values from -40 to 40
- ssm_gate: bfloat16 [2048, 8192], P('ctx', 'tp'), may hold values from -4 to 4
- state_write: bfloat16 [2048, 128], P('ctx'), may hold values from -0.5 to 0.5
- state_read: bfloat16 [2048, 128], P('ctx'), may hold values from -0.5 to 0.5
- log_decay: float32 [2048, 32], P('ctx', 'tp'), may hold values from -4 to 0
- skip_gain: float32 [32], P('tp'), may hold values from 0.5 to 1.5
- norm_gain: float32 [8192], P('tp'), may hold values from 0.1 to 1.9
- ssm_cotangent: bfloat16 [2048, 8192], P('ctx', 'tp'), may hold values from -6 to 6
- queries: bfloat16 [2048, 8192], P('ctx', 'tp'), may hold values from -5 to 5
- key_states: bfloat16 [2048, 1024], P('ctx', 'tp'), may hold values from -5 to 5
- value_states: bfloat16 [2048, 1024], P('ctx', 'tp'), may hold values from -6 to 6
- attn_cotangent: bfloat16 [2048, 8192], P('ctx', 'tp'), may hold values from -6 to 6
Outputs:
- ssm_output: bfloat16 [2048, 8192], P('ctx', 'tp')
- input_grad: bfloat16 [2048, 8192], P('ctx', 'tp')
- gate_grad: bfloat16 [2048, 8192], P('ctx', 'tp')
- write_grad: float32 [2048, 128], P('ctx')
- read_grad: float32 [2048, 128], P('ctx')
- attn_output: bfloat16 [2048, 8192], P('ctx', 'tp')
- query_grad: bfloat16 [2048, 8192], P('ctx', 'tp')
- key_grad: bfloat16 [2048, 1024], P('ctx', 'tp')
- value_grad: bfloat16 [2048, 1024], P('ctx', 'tp')
All inputs are finite; a program needn't handle non-finite values.
Results may differ from a plain program's by a relative error of at most 0.035.
Values may be sent and summed in bfloat16 or wider, within the bound.
A program may use at most 192 MiB of HBM per device.

v0:
```python
import jax
import jax.numpy as jnp
from jax import lax
from jax.sharding import PartitionSpec as P

HD = 128
CH = 8192


PRECISE = lax.Precision.HIGHEST
NEGATIVE = -1e30
EPSILON = 1e-05
TILE_KEYS = 1024


def carried_in(x, axis, join, neutral, backward):
    count = lax.axis_size(axis)
    place = lax.axis_index(axis)
    ahead = count - 1 - place if backward else place
    gathered = jax.tree.map(
        lambda a, kind: lax.all_gather(a.astype(kind), axis),
        x,
        jax.tree.map(lambda a: jnp.bfloat16 if a.dtype == jnp.float32 else a.dtype, x),
    )
    state = jax.tree.map(lambda a, e: jnp.zeros_like(a) + jnp.asarray(e, a.dtype), x, neutral)

    def one(turn, state):
        source = count - 1 - turn if backward else turn
        return join(
            state,
            jax.tree.map(
                lambda a, own: lax.dynamic_index_in_dim(a, source, 0, False).astype(own.dtype),
                gathered,
                x,
            ),
        )

    return lax.fori_loop(0, ahead, one, state)


def for_sending(x):

    def short(part):
        return part.astype(jnp.bfloat16) if part.dtype == jnp.float32 else part

    return jax.tree.map(short, x)


def spread(value, axis, source):
    kept = jnp.where(lax.axis_index(axis) == source, value, 0).astype(value.dtype)
    return lax.psum(kept, axis)


def combine(earlier, latter):
    return (earlier[0] * latter[0], latter[0][:, None, None] * earlier[1] + latter[1])


def carried(leading, trailing):
    neutral = (jnp.ones_like(leading[0]), jnp.zeros_like(leading[1]))
    before_state = carried_in(leading, "ctx", combine, neutral, False)
    through = combine(before_state, leading)
    total_state = spread(for_sending(through[1]), "ctx", lax.axis_size("ctx") - 1)
    after_state = carried_in(trailing, "ctx", combine, neutral, True)
    entering = after_state[0][:, None, None] * total_state + after_state[1]
    return (before_state[1], entering)


def ssm_layer(
    ssm_input, ssm_gate, state_write, state_read, log_decay, skip_gain, norm_gain, ssm_cotangent
):
    tok_rows, channel_count = ssm_input.shape
    head_count = log_decay.shape[1]
    half_rows = tok_rows // 2
    head_dim = channel_count // head_count
    input_f32 = ssm_input.astype(jnp.float32).reshape(2, half_rows, head_count, head_dim)
    write_pair = state_write.reshape(2, half_rows, -1)
    read_pair = state_read.reshape(2, half_rows, -1)
    write_f32 = write_pair.astype(jnp.float32)
    read_f32 = read_pair.astype(jnp.float32)
    log_total = jnp.cumsum(log_decay.reshape(2, half_rows, head_count), axis=1)
    by_head = jnp.transpose(log_total, (0, 2, 1))
    log_gap = by_head[:, :, :, None] - by_head[:, :, None, :]
    causal = lax.broadcasted_iota(jnp.int32, (half_rows, half_rows), 0) >= lax.broadcasted_iota(
        jnp.int32, (half_rows, half_rows), 1
    )
    decay = jnp.exp(jnp.where(causal, log_gap, NEGATIVE))
    read_write = jnp.einsum(
        "ctn,csn->cts", read_pair, write_pair, preferred_element_type=jnp.float32
    )
    weights = decay * read_write[:, None, :, :]
    grow_in = jnp.exp(log_total)
    log_last = log_total[:, -1, :]
    shrink = jnp.exp(log_last[:, None, :] - log_total)
    block_decay = jnp.exp(log_last)
    local_state = jnp.einsum(
        "cshp,csn->chpn", input_f32 * shrink[..., None], write_f32, precision=PRECISE
    )
    first_in, second_in = carried(
        (block_decay[0], local_state[0]), (block_decay[1], local_state[1])
    )
    state_in = jnp.stack([first_in, second_in])
    mixed = jnp.einsum("chts,cshp->cthp", weights, input_f32, precision=PRECISE)
    mixed = mixed + grow_in[..., None] * jnp.einsum(
        "chpn,ctn->cthp", state_in, read_f32, precision=PRECISE
    )
    mixed = mixed + skip_gain[None, None, :, None] * input_f32
    mixed = mixed.reshape(tok_rows, channel_count)
    gate_f32 = ssm_gate.astype(jnp.float32)
    sigmoid_gate = jax.nn.sigmoid(gate_f32)
    gated = mixed * gate_f32 * sigmoid_gate
    square_sum = lax.psum(jnp.sum(gated * gated, axis=1), "tp")
    root_mean = jnp.sqrt(square_sum / CH + EPSILON)[:, None]
    normed = gated / root_mean
    ssm_output = (normed * norm_gain).astype(jnp.bfloat16)
    d_normed = ssm_cotangent.astype(jnp.float32) * norm_gain
    inner_sum = lax.psum(jnp.sum(d_normed * normed, axis=1), "tp")
    d_gated = (d_normed - normed * (inner_sum / CH)[:, None]) / root_mean
    d_mixed_flat = d_gated * gate_f32 * sigmoid_gate
    gate_grad = (d_gated * mixed * sigmoid_gate * (1.0 + gate_f32 * (1.0 - sigmoid_gate))).astype(
        jnp.bfloat16
    )
    d_mixed = d_mixed_flat.reshape(2, half_rows, head_count, head_dim)
    local_adjoint = jnp.einsum(
        "cshp,csn->chpn", d_mixed * grow_in[..., None], read_f32, precision=PRECISE
    )
    second_back, first_back = carried(
        (block_decay[1], local_adjoint[1]), (block_decay[0], local_adjoint[0])
    )
    adjoint_in = jnp.stack([first_back, second_back])
    input_g = jnp.einsum("chst,cshp->cthp", weights, d_mixed, precision=PRECISE)
    input_g = input_g + shrink[..., None] * jnp.einsum(
        "chpn,ctn->cthp", adjoint_in, write_f32, precision=PRECISE
    )
    input_g = input_g + skip_gain[None, None, :, None] * d_mixed
    input_grad = input_g.reshape(tok_rows, channel_count).astype(jnp.bfloat16)
    dot_pairs = jnp.einsum("cthp,cshp->chts", d_mixed, input_f32, precision=PRECISE)
    kernel = jnp.sum(decay * dot_pairs, axis=1)
    read_g = jnp.einsum("cts,csn->ctn", kernel, write_f32, precision=PRECISE)
    read_g = read_g + jnp.einsum(
        "cthp,chpn->ctn", d_mixed * grow_in[..., None], state_in, precision=PRECISE
    )
    write_g = jnp.einsum("cst,csn->ctn", kernel, read_f32, precision=PRECISE)
    write_g = write_g + jnp.einsum(
        "cthp,chpn->ctn", input_f32 * shrink[..., None], adjoint_in, precision=PRECISE
    )
    write_grad, read_grad = (
        lax.psum(write_g.reshape(tok_rows, -1).astype(jnp.bfloat16), "tp").astype(jnp.float32),
        lax.psum(read_g.reshape(tok_rows, -1).astype(jnp.bfloat16), "tp").astype(jnp.float32),
    )
    return (ssm_output, input_grad, gate_grad, write_grad, read_grad)


def pick_half(values, half_id):
    return lax.dynamic_index_in_dim(values, half_id, 0, keepdims=False)


def take_half(tree, half_id):
    return jax.tree.map(lambda values: pick_half(values, half_id), tree)


def put_half(tree, half_id, update_tree):
    return jax.tree.map(
        lambda values, replacement: lax.dynamic_update_index_in_dim(
            values, replacement, half_id, 0
        ),
        tree,
        update_tree,
    )


def add_rows(totals, update_rows, row_start):
    current = lax.dynamic_slice_in_dim(totals, row_start, update_rows.shape[0], 0)
    return lax.dynamic_update_slice_in_dim(totals, current + update_rows, row_start, 0)


def score_block(query_block, key_block, key_mask, score_scale):
    raw_scores = (
        jnp.einsum("tkgd,skd->kgts", query_block, key_block, preferred_element_type=jnp.float32)
        * score_scale
    )
    return jnp.where(key_mask, raw_scores, NEGATIVE)


def absorb(soft_state, query_block, key_block, value_block, key_mask, score_scale):
    row_max, weight_sum, accum_out = soft_state
    scores = score_block(query_block, key_block, key_mask, score_scale)
    new_max = jnp.maximum(row_max, jnp.max(scores, axis=-1))
    rescale = jnp.exp(row_max - new_max)
    prob_full = jnp.exp(scores - new_max[..., None])
    accum_out = accum_out * rescale[..., None] + jnp.einsum(
        "kgts,skd->kgtd",
        prob_full.astype(jnp.bfloat16),
        value_block,
        preferred_element_type=jnp.float32,
    )
    return (new_max, weight_sum * rescale + jnp.sum(prob_full, axis=-1), accum_out)


def grad_block(
    query_block, key_block, value_block, cot_block, norm_block, delta_block, key_mask, score_scale
):
    scores = score_block(query_block, key_block, key_mask, score_scale)
    prob_full = jnp.exp(scores - norm_block[..., None])
    weights = prob_full.astype(jnp.bfloat16)
    d_prob = jnp.einsum(
        "tkgd,skd->kgts", cot_block, value_block, preferred_element_type=jnp.float32
    )
    d_score = (prob_full * (d_prob - delta_block[..., None]) * score_scale).astype(jnp.bfloat16)
    query_g = jnp.einsum("kgts,skd->tkgd", d_score, key_block, preferred_element_type=jnp.float32)
    key_g = jnp.einsum("kgts,tkgd->skd", d_score, query_block, preferred_element_type=jnp.float32)
    value_g = jnp.einsum("kgts,tkgd->skd", weights, cot_block, preferred_element_type=jnp.float32)
    return (query_g, key_g, value_g)


def key_positions(first_row, row_count, tok_rows, half_rows, ctx_count):
    row_id = first_row + lax.iota(jnp.int32, row_count)
    device_id = row_id // tok_rows
    local_id = row_id % tok_rows
    block_id = jnp.where(local_id < half_rows, device_id, 2 * ctx_count - 1 - device_id)
    return block_id * half_rows + local_id % half_rows


def over_pieces(by_rows, carry, pieces, tok_rows):
    row_count = pieces[0].shape[0]
    shards = row_count // tok_rows
    group = 1
    for candidate in range(1, shards + 1):
        if shards % candidate == 0 and candidate * tok_rows <= TILE_KEYS:
            group = candidate
    tile_rows = group * tok_rows

    def tile_turn(offset, inner_carry):
        key_rows = lax.dynamic_slice_in_dim(pieces[0], offset * tile_rows, tile_rows, 0)
        value_rows = lax.dynamic_slice_in_dim(pieces[1], offset * tile_rows, tile_rows, 0)
        return by_rows(inner_carry, key_rows, value_rows, offset * tile_rows)

    return lax.fori_loop(0, shards // group, tile_turn, carry)


def attention(queries, key_states, value_states, attn_cotangent):
    tok_rows = queries.shape[0]
    half_rows = tok_rows // 2
    kv_count = key_states.shape[1] // HD
    group_size = queries.shape[1] // HD // kv_count
    score_scale = HD ** (-0.5)
    ctx_count = lax.axis_size("ctx")
    own_index = lax.axis_index("ctx")
    query_pair = queries.reshape(2, half_rows, kv_count, group_size, HD)
    cot_pair = attn_cotangent.reshape(2, half_rows, kv_count, group_size, HD)
    block_starts = jnp.stack([own_index, 2 * ctx_count - 1 - own_index]) * half_rows
    query_pos = block_starts[:, None] + lax.iota(jnp.int32, half_rows)[None, :]

    def forward_rows(soft_state, key_rows, value_rows, first_row):
        row_count = key_rows.shape[0]
        key_pos = key_positions(first_row, row_count, tok_rows, half_rows, ctx_count)
        key_block = key_rows.reshape(row_count, kv_count, HD)
        value_block = value_rows.reshape(row_count, kv_count, HD)
        for half_id in range(2):
            key_mask = key_pos[None, :] <= query_pos[half_id][:, None]
            soft_state = put_half(
                soft_state,
                half_id,
                absorb(
                    take_half(soft_state, half_id),
                    query_pair[half_id],
                    key_block,
                    value_block,
                    key_mask,
                    score_scale,
                ),
            )
        return soft_state

    start_state = (
        jnp.full((2, kv_count, group_size, half_rows), NEGATIVE, jnp.float32),
        jnp.zeros((2, kv_count, group_size, half_rows), jnp.float32),
        jnp.zeros((2, kv_count, group_size, half_rows, HD), jnp.float32),
    )
    row_max, weight_sum, accum_out = over_pieces(
        forward_rows,
        start_state,
        (
            lax.all_gather(key_states, "ctx", axis=0, tiled=True),
            lax.all_gather(value_states, "ctx", axis=0, tiled=True),
        ),
        tok_rows,
    )
    out_pair = jnp.transpose(accum_out / weight_sum[..., None], (0, 3, 1, 2, 4))
    attn_output = out_pair.reshape(tok_rows, -1).astype(jnp.bfloat16)
    norm_pair = row_max + jnp.log(weight_sum)
    delta_rows = jnp.sum(
        attn_output.reshape(2, half_rows, kv_count, group_size, HD).astype(jnp.float32)
        * cot_pair.astype(jnp.float32),
        axis=-1,
    )
    delta_pair = jnp.transpose(delta_rows, (0, 2, 3, 1))

    def backward_rows(carry, key_rows, value_rows, first_row):
        row_count = key_rows.shape[0]
        key_pos = key_positions(first_row, row_count, tok_rows, half_rows, ctx_count)
        key_block = key_rows.reshape(row_count, kv_count, HD)
        value_block = value_rows.reshape(row_count, kv_count, HD)
        dq_pair, dk_all, dv_all = carry
        for half_id in range(2):
            key_mask = key_pos[None, :] <= query_pos[half_id][:, None]
            block_grads = grad_block(
                query_pair[half_id],
                key_block,
                value_block,
                cot_pair[half_id],
                norm_pair[half_id],
                delta_pair[half_id],
                key_mask,
                score_scale,
            )
            dq_pair = dq_pair.at[half_id].add(block_grads[0])
            dk_all = add_rows(dk_all, block_grads[1], first_row)
            dv_all = add_rows(dv_all, block_grads[2], first_row)
        return (dq_pair, dk_all, dv_all)

    all_rows = tok_rows * ctx_count
    grad_start = (
        jnp.zeros((2, half_rows, kv_count, group_size, HD), jnp.float32),
        jnp.zeros((all_rows, kv_count, HD), jnp.float32),
        jnp.zeros((all_rows, kv_count, HD), jnp.float32),
    )
    dq_pair, dk_all, dv_all = over_pieces(
        backward_rows,
        grad_start,
        (
            lax.all_gather(key_states, "ctx", axis=0, tiled=True),
            lax.all_gather(value_states, "ctx", axis=0, tiled=True),
        ),
        tok_rows,
    )
    dk_mine, dv_mine = (
        lax.psum_scatter(
            dk_all.astype(jnp.bfloat16), "ctx", scatter_dimension=0, tiled=True
        ).astype(jnp.float32),
        lax.psum_scatter(
            dv_all.astype(jnp.bfloat16), "ctx", scatter_dimension=0, tiled=True
        ).astype(jnp.float32),
    )
    query_grad = dq_pair.reshape(tok_rows, -1).astype(jnp.bfloat16)
    key_grad = dk_mine.reshape(tok_rows, -1).astype(jnp.bfloat16)
    value_grad = dv_mine.reshape(tok_rows, -1).astype(jnp.bfloat16)
    return (attn_output, query_grad, key_grad, value_grad)


def per_device(
    ssm_input,
    ssm_gate,
    state_write,
    state_read,
    log_decay,
    skip_gain,
    norm_gain,
    ssm_cotangent,
    queries,
    key_states,
    value_states,
    attn_cotangent,
):
    ssm_results = ssm_layer(
        ssm_input, ssm_gate, state_write, state_read, log_decay, skip_gain, norm_gain, ssm_cotangent
    )
    attn_results = attention(queries, key_states, value_states, attn_cotangent)
    return ssm_results + attn_results


def solution(mesh):
    placed = (
        P("ctx", "tp"),
        P("ctx", "tp"),
        P("ctx", None),
        P("ctx", None),
        P("ctx", "tp"),
        P("tp"),
        P("tp"),
        P("ctx", "tp"),
        P("ctx", "tp"),
        P("ctx", "tp"),
        P("ctx", "tp"),
        P("ctx", "tp"),
    )
    return jax.shard_map(
        per_device,
        mesh=mesh,
        in_specs=placed,
        out_specs=(
            P("ctx", "tp"),
            P("ctx", "tp"),
            P("ctx", "tp"),
            P("ctx", None),
            P("ctx", None),
            P("ctx", "tp"),
            P("ctx", "tp"),
            P("ctx", "tp"),
            P("ctx", "tp"),
        ),
        check_vma=False,
    )
```

profile of v0, /device:TPU:0, one launch (start us, length us, event | category | flops | bytes accessed | tf_op | source)
XLA Modules:
  0.0 1338.5 jit_solution(10396937734925266200)
XLA Ops:
  13.3 3.8 fusion.126
  21.1 42.3 %all-gather = bf16[16,1,16]{2,1,0:T(2,128)(2,1)S(1)} all-gather(bf16[1,1,16]{2,1,0:T(2,128)(2,1)S(1)} %get-tuple-element.1035), channel_id=1, replica_groups=mesh['ctx'=16,'tp'=2] {'ctx'}, dimensions={0}, use_global_device_ids=true | all-gather | bytes 544 | tf_op jit(solution)/shard_map/all_gather | solution.py:21
  68.1 9.3 all-gather.17.cloned.1.call-done
  77.4 64.8 %all-gather.19.cloned.1.call-done = bf16[2048,512]{0,1:T(8,128)(2,1)} async-done(((bf16[128,512]{0,1:T(8,128)(2,1)}), bf16[2048,512]{0,1:T(8,128)(2,1)}) %all-gather.19.cloned.1.call-update) | async-done | bytes 2097168 | tf_op jit(solution)/shard_map/all_gather | solution.py:284
  142.4 28.8 %while.98 = (s32[]{:T(128)}, f32[2,4,8,64]{3,2,1,0:T(8,128)S(1)}, f32[2,4,8,64]{3,2,1,0:T(8,128)S(1)}, f32[2,4,8,64,128]{4,3,2,1,0:T(8,128)S(1)}, s32[2,64]{1,0:...) while((s32[]{:T(128)}, f32[2,4,8,64]{3,2,1,0:T(8,128)S(1)}, ...), condition=%wide.region_23.24_spmd, body=%wide.region_18.23_spmd.sunk | while | flops 2194853888 | bytes 69060272 | solution.py:237
  172.0 4.3 multiply_reduce_fusion
  178.0 157.3 %all-gather.9.cloned.1.call-done = bf16[16,16,256,128]{3,2,1,0:T(8,128)(2,1)} async-done(((bf16[1,16,256,128]{3,2,1,0:T(8,128)(2,1)}), bf16[16,16,256,128]{3,2,1,0:T(8,128)(2,1)}) %all-gather.9.cloned.1.call-update) | async-done | bytes 16777232 | tf_op jit(solution)/shard_map/all_gather | solution.py:21
  335.5 3.7 fusion.164
  344.1 75.8 %while.99 = (s32[]{:T(128)}, f32[2,64,4,8,128]{4,1,3,2,0:T(8,128)S(1)}, f32[2048,4,128]{2,0,1:T(8,128)}, f32[2048,4,128]{2,0,1:T(8,128)}, bf16[2048,512]{0,1:T(8...) while((s32[]{:T(128)}, ...), condition=%wide.region_26.27_spmd, body=%wide.region_25.26_spmd.sunk | while | flops 5417635840 | bytes 150054832 | solution.py:237
  374.2 7.5 fusion.328
  381.7 5.9 fusion.329
  406.1 7.5 fusion.328
  413.6 5.9 fusion.329
  419.9 3.8 convert_element_type.295
  424.6 68.4 %all-gather.1 = bf16[16,1,16]{2,1,0:T(2,128)(2,1)S(1)} all-gather(bf16[1,1,16]{2,1,0:T(2,128)(2,1)S(1)} %copy-done.38), channel_id=1, replica_groups=mesh['ctx'=16,'tp'=2] {'ctx'}, dimensions={0}, use_global_device_ids=true | all-gather | bytes 544 | tf_op jit(solution)/shard_map/all_gather | solution.py:21
  496.0 4.0 convert_element_type.297
  500.1 28.4 %all-gather.11.cloned.1.call-done = bf16[16,16,256,128]{3,2,1,0:T(8,128)(2,1)} async-done(((bf16[1,16,256,128]{3,2,1,0:T(8,128)(2,1)}), bf16[16,16,256,128]{3,2,1,0:T(8,128)(2,1)}) %all-gather.11.cloned.1.call-update) | async-done | bytes 16777232 | tf_op jit(solution)/shard_map/all_gather | solution.py:21
  530.1 53.4 %while.95 = (s32[]{:T(128)}, f32[16]{0:T(128)S(1)}, f32[16,256,128]{2,1,0:T(8,128)}, s32[]{:T(128)}, bf16[16,16]{1,0:T(8,128)(2,1)S(1)}, /*index=5*/bf16[16,16,2...) while((s32[]{:T(128)}, f32[16]{0:T(128)S(1)}, f32[16,256,128]{2,1,0:T(8,128)}, ...), condition=%wide.region_4.5_spmd, body=%wide.region_3.4_spmd.sunk | while | flops 1572902 | bytes 5243331 | solution.py:38
  583.5 60.7 %all-reduce.5.cloned.1.call-done = bf16[16,256,128]{2,1,0:T(8,128)(2,1)} async-done(((bf16[16,256,128]{2,1,0:T(8,128)(2,1)}), bf16[16,256,128]{2,1,0:T(8,128)(2,1)}) %all-reduce.5.cloned.1.call-update) | async-done | bytes 1048592 | tf_op jit(solution)/shard_map/psum | solution.py:51
  658.1 4.1 multiply_reduce_fusion.1
  664.7 5.2 fusion.135
  671.9 4.4 fusion.144
  683.7 42.2 %reduce-scatter.3.cloned.1.call-done = bf16[128,4,128]{2,0,1:T(8,128)(2,1)} async-done(((bf16[2048,4,128]{2,0,1:T(8,128)(2,1)}), bf16[128,4,128]{2,0,1:T(8,128)(2,1)}) %reduce-scatter.3.cloned.1.call-update) | async-done | bytes 131088 | tf_op jit(solution)/shard_map/reduce_scatter | solution.py:337
  727.4 78.4 %reduce-scatter.5.cloned.1.call-done = bf16[128,4,128]{2,0,1:T(8,128)(2,1)} async-done(((bf16[2048,4,128]{2,0,1:T(8,128)(2,1)}), bf16[128,4,128]{2,0,1:T(8,128)(2,1)}) %reduce-scatter.5.cloned.1.call-update) | async-done | bytes 131088 | tf_op jit(solution)/shard_map/reduce_scatter | solution.py:340
  807.4 6.1 fusion.158
  816.9 4.7 fusion.150
  821.6 175.9 %all-gather.15.cloned.1.call-done = bf16[16,16,256,128]{3,2,1,0:T(8,128)(2,1)} async-done(((bf16[1,16,256,128]{3,2,1,0:T(8,128)(2,1)}), bf16[16,16,256,128]{3,2,1,0:T(8,128)(2,1)}) %all-gather.15.cloned.1.call-update) | async-done | bytes 16777232 | tf_op jit(solution)/shard_map/all_gather | solution.py:21
  1001.4 188.7 %all-gather.13.cloned.1.call-done = bf16[16,16,256,128]{3,2,1,0:T(8,128)(2,1)} async-done(((bf16[1,16,256,128]{3,2,1,0:T(8,128)(2,1)}), bf16[16,16,256,128]{3,2,1,0:T(8,128)(2,1)}) %all-gather.13.cloned.1.call-update) | async-done | bytes 16777232 | tf_op jit(solution)/shard_map/all_gather | solution.py:21
  1191.6 63.5 %while.96 = (s32[]{:T(128)}, f32[16]{0:T(128)S(1)}, f32[16,256,128]{2,1,0:T(8,128)}, s32[]{:T(128)}, bf16[16,16]{1,0:T(8,128)(2,1)}, /*index=5*/bf16[16,16,256,1...) while((s32[]{:T(128)}, f32[16]{0:T(128)S(1)}, f32[16,256,128]{2,1,0:T(8,128)}, ...), condition=%wide.region_11.12_spmd, body=%wide.region_10.11_spmd.sunk | while | flops 1572902 | bytes 5243331 | solution.py:38
  1255.1 50.6 %all-reduce.7.cloned.1.call-done = bf16[16,256,128]{2,1,0:T(8,128)(2,1)} async-done(((bf16[16,256,128]{2,1,0:T(8,128)(2,1)}), bf16[16,256,128]{2,1,0:T(8,128)(2,1)}) %all-reduce.7.cloned.1.call-update) | async-done | bytes 1048592 | tf_op jit(solution)/shard_map/psum | solution.py:51
  1312.0 6.3 fusion.138
  1320.3 8.7 all-reduce.9.cloned.1.call-done
  (301 shorter events, 258.0 us)
Async XLA Ops:
  7.2 486.0 %copy-start = (bf16[128,128]{1,0:T(8,128)(2,1)S(1)}, bf16[128,128]{1,0:T(8,128)(2,1)}, u32[]{:S(2)}) copy-start(bf16[128,128]{1,0:T(8,128)(2,1)} %param.31) | copy-start | bytes 98308
  7.2 5.0 copy-start.36
  7.2 6.1 copy-start.26
  7.2 70.1 %all-gather.17.cloned.1.call-start = ((), (), s32[]{:S(2)}) async-start(), calls=%async_computation.8 | async-start | bytes 2228224 | tf_op jit(solution)/shard_map/all_gather | solution.py:283
  8.9 133.2 %all-gather.19.cloned.1.call-start = ((), (), s32[]{:S(2)}) async-start(), calls=%async_computation.9 | async-start | bytes 2228224 | tf_op jit(solution)/shard_map/all_gather | solution.py:284
  10.7 324.6 %all-gather.9.cloned.1.call-start = ((), (), s32[]{:S(2)}) async-start(), calls=%async_computation.2 | async-start | bytes 17825792 | tf_op jit(solution)/shard_map/all_gather | solution.py:21
  12.2 4.9 copy-start.9
  12.4 4.7 copy-start.24
  13.3 3.8 copy-start.30
  19.8 43.6 %copy-start.22 = (bf16[128,4096]{1,0:T(8,128)(2,1)S(1)}, bf16[128,4096]{1,0:T(8,128)(2,1)}, u32[]{:S(2)}) copy-start(bf16[128,4096]{1,0:T(8,128)(2,1)} %param.39) | copy-start | bytes 3145732
  19.8 508.7 %all-gather.11.cloned.1.call-start = ((), (), s32[]{:S(2)}) async-start(), calls=%async_computation.3 | async-start | bytes 17825792 | tf_op jit(solution)/shard_map/all_gather | solution.py:21
  20.4 623.8 %all-reduce.5.cloned.1.call-start = ((), (), s32[]{:S(2)}) async-start(), calls=%async_computation.4 | async-start | bytes 2097152 | tf_op jit(solution)/shard_map/psum | solution.py:51
  339.3 386.5 %reduce-scatter.3.cloned.1.call-start = ((), (), s32[]{:S(2)}) async-start(), calls=%async_computation.10 | async-start | bytes 2228224 | tf_op jit(solution)/shard_map/reduce_scatter | solution.py:337
  359.5 5.9 copy-start.28
  359.7 5.7 copy-start.20
  374.2 7.5 copy-start.2
  391.4 5.9 copy-start.28
  391.6 5.8 copy-start.20
  406.1 7.5 copy-start.2
  423.7 69.4 %copy-start.32 = (f32[2,64,16]{2,1,0:T(8,128)S(1)}, f32[2,64,16]{2,1,0:T(8,128)}, u32[]{:S(2)}) copy-start(f32[2,64,16]{2,1,0:T(8,128)} %get-tuple-element.1031) | copy-start | bytes 24580
  423.7 69.4 %copy-start.27 = (bf16[128,128]{1,0:T(8,128)(2,1)S(1)}, bf16[128,128]{1,0:T(8,128)(2,1)}, u32[]{:S(2)}) copy-start(bf16[128,128]{1,0:T(8,128)(2,1)} %param.30) | copy-start | bytes 98308
  423.7 69.6 %copy-start.10 = (bf16[16,8,16,256]{3,2,1,0:T(8,128)(2,1)S(1)}, bf16[16,8,16,256]{3,2,1,0:T(8,128)(2,1)}, u32[]{:S(2)}) copy-start(bf16[16,8,16,256]{3,2,1,0:T(8,128)(2,1)} %copy-done.9) | copy-start | bytes 3145732
  423.8 382.1 %reduce-scatter.5.cloned.1.call-start = ((), (), s32[]{:S(2)}) async-start(), calls=%async_computation.11 | async-start | bytes 2228224 | tf_op jit(solution)/shard_map/reduce_scatter | solution.py:340
  500.0 497.4 %all-gather.15.cloned.1.call-start = ((), (), s32[]{:S(2)}) async-start(), calls=%async_computation.6 | async-start | bytes 17825792 | tf_op jit(solution)/shard_map/all_gather | solution.py:21
  646.5 4.1 copy-start.12
  653.5 4.6 copy-start.33
  679.1 511.0 %all-gather.13.cloned.1.call-start = ((), (), s32[]{:S(2)}) async-start(), calls=%async_computation.5 | async-start | bytes 17825792 | tf_op jit(solution)/shard_map/all_gather | solution.py:21
  679.8 625.9 %all-reduce.7.cloned.1.call-start = ((), (), s32[]{:S(2)}) async-start(), calls=%async_computation.7 | async-start | bytes 2097152 | tf_op jit(solution)/shard_map/psum | solution.py:51
  681.7 125.7 %copy-start.5 = (f32[16,256,128]{2,1,0:T(8,128)S(1)}, f32[16,256,128]{2,1,0:T(8,128)}, u32[]{:S(2)}) copy-start(f32[16,256,128]{2,1,0:T(8,128)} %copy-done.3) | copy-start | bytes 6291460
  807.4 6.1 copy-start.7
  807.4 6.1 copy-start.11
  1001.3 327.6 %all-reduce.9.cloned.1.call-start = ((), (), s32[]{:S(2)}) async-start(), calls=%async_computation.12 | async-start | bytes 131072 | tf_op jit(solution)/shard_map/psum | solution.py:147
  (25 other events, 60.6 us)
Sparse Core Ops, SparseCore 0:
  11.3 65.9 all-gather.16
  80.6 61.4 all-gather.18
  145.5 189.7 all-gather.8
  338.5 189.9 all-gather.10
  534.2 109.9 all-reduce.4
  646.3 79.4 reduce-scatter.2
  728.1 77.6 reduce-scatter.4
  808.6 188.8 all-gather.14
  1000.2 189.7 all-gather.12
  1195.8 109.9 all-reduce.6
  1312.1 16.8 all-reduce.8
where the time goes:
time: 1350 us; the launch traced here: 1340 us
  waiting for transfers between devices  866 us (64%)
  other arithmetic  165 us (12%)
  blocking collectives  116 us (9%)
  matrix products  110 us (8%)
  local copies, waits for them, and re-layouts  53.2 us (4%)
  between operations  14.6 us (1%)
    all_gather x4, waiting for transfers between devices, carried_in(): lax.all_gather(a.astype(kind), axis)  550 us
    psum x2, waiting for transfers between devices, spread(): return lax.psum(kept, axis)  111 us
    all_gather x2, blocking collectives, carried_in(): lax.all_gather(a.astype(kind), axis)  111 us
    add x30, other arithmetic, combine(): latter[0][:, None, None] * earlier[1] + latter[1]  106 us
    reduce_scatter x1, waiting for transfers between devices, attention(): lax.psum_scatter(dv_all.astype(jnp.bfloat16), 'ctx', scatter_dimension=0,...  78.4 us
    all_gather x1, waiting for transfers between devices, attention(): lax.all_gather(value_states, 'ctx', axis=0, tiled=True)  64.8 us
    reduce_scatter x1, waiting for transfers between devices, attention(): lax.psum_scatter(dk_all.astype(jnp.bfloat16), 'ctx', scatter_dimension=0,...  42.2 us
  transfers between devices with their start and end apart: 11, of which 11 were waited for; matrix products, arithmetic and copies ran while one was open for 23% of the time, Pallas kernels for 0%

commit v1 on v0

v1 whole, which is shorter than its diff:
```python
import functools

import jax
import jax.numpy as jnp
from jax import lax
from jax.experimental import pallas as pl
from jax.experimental.pallas import tpu as pltpu
from jax.sharding import PartitionSpec as P

HD = 128
CH = 8192
PRECISE = lax.Precision.HIGHEST
NEGATIVE = -1e30
EPSILON = 1e-05
TILE_KEYS = 256
CHUNK = 256
VMEM_BYTES = 48 * 1024 * 1024


def dot(a, b, a_dim, b_dim):
    return lax.dot_general(
        a, b, (((a_dim,), (b_dim,)), ((), ())), preferred_element_type=jnp.float32
    )


def attention_kernel(
    place_ref, q_ref, kv_ref, cot_ref, out_ref, dq_ref, dkv_ref,
    keys, values, dk_sum, dv_sum, scores, q_rows, cot_rows, acc,
):
    count, _, _, half_rows, _ = kv_ref.shape
    group = q_ref.shape[1] // HD
    rows = group * half_rows
    scale = HD ** (-0.5)
    place = place_ref[0]
    for j in range(count):
        near = pl.ds(j * half_rows, half_rows)
        far = pl.ds((2 * count - 1 - j) * half_rows, half_rows)
        keys[near] = kv_ref[j, 0, 0]
        keys[far] = kv_ref[j, 0, 1]
        values[near] = kv_ref[j, 1, 0]
        values[far] = kv_ref[j, 1, 1]
    dk_sum[...] = jnp.zeros_like(dk_sum)
    dv_sum[...] = jnp.zeros_like(dv_sum)
    for half in range(2):
        block = place if half == 0 else 2 * count - 1 - place
        tiles = block // (TILE_KEYS // half_rows) + 1
        for h in range(group):
            there = (pl.ds(half * half_rows, half_rows), pl.ds(h * HD, HD))
            q_rows[pl.ds(h * half_rows, half_rows)] = q_ref[there]
            cot_rows[pl.ds(h * half_rows, half_rows)] = cot_ref[there]
        q_pos = block * half_rows + lax.broadcasted_iota(jnp.int32, (1, rows), 1) % half_rows

        def score_turn(tile, top):
            at = pl.ds(pl.multiple_of(tile * TILE_KEYS, TILE_KEYS), TILE_KEYS)
            s = dot(keys[at], q_rows[...], 1, 1) * scale
            key_pos = tile * TILE_KEYS + lax.broadcasted_iota(jnp.int32, s.shape, 0)
            s = jnp.where(key_pos <= q_pos, s, NEGATIVE)
            scores[at] = s
            return jnp.maximum(top, jnp.max(s, axis=0, keepdims=True))

        top = lax.fori_loop(0, tiles, score_turn, jnp.full((1, rows), NEGATIVE, jnp.float32))
        acc[...] = jnp.zeros_like(acc)

        def value_turn(tile, total):
            at = pl.ds(pl.multiple_of(tile * TILE_KEYS, TILE_KEYS), TILE_KEYS)
            p = jnp.exp(scores[at] - top)
            scores[at] = p
            acc[...] += dot(values[at], p.astype(jnp.bfloat16), 0, 0)
            return total + jnp.sum(p, axis=0, keepdims=True)

        total = lax.fori_loop(0, tiles, value_turn, jnp.zeros((1, rows), jnp.float32))
        inverse = 1.0 / total
        out_t = acc[...] * inverse
        out_rows = out_t.T.astype(jnp.bfloat16)
        cot_t = cot_rows[...].astype(jnp.float32).T
        delta = jnp.sum(
            cot_t * out_t.astype(jnp.bfloat16).astype(jnp.float32), axis=0, keepdims=True
        )
        acc[...] = jnp.zeros_like(acc)

        def grad_turn(tile, carry):
            at = pl.ds(pl.multiple_of(tile * TILE_KEYS, TILE_KEYS), TILE_KEYS)
            w = scores[at] * inverse
            d_prob = dot(values[at], cot_rows[...], 1, 1)
            d_score = (w * (d_prob - delta) * scale).astype(jnp.bfloat16)
            acc[...] += dot(keys[at], d_score, 0, 0)
            dk_sum[at] += dot(d_score, q_rows[...], 1, 0)
            dv_sum[at] += dot(w.astype(jnp.bfloat16), cot_rows[...], 1, 0)
            return carry

        lax.fori_loop(0, tiles, grad_turn, 0)
        dq_rows = acc[...].T.astype(jnp.bfloat16)
        for h in range(group):
            there = (pl.ds(half * half_rows, half_rows), pl.ds(h * HD, HD))
            out_ref[there] = out_rows[h * half_rows : (h + 1) * half_rows]
            dq_ref[there] = dq_rows[h * half_rows : (h + 1) * half_rows]
    for j in range(count):
        near = pl.ds(j * half_rows, half_rows)
        far = pl.ds((2 * count - 1 - j) * half_rows, half_rows)
        dkv_ref[j, 0, 0] = dk_sum[near].astype(jnp.bfloat16)
        dkv_ref[j, 0, 1] = dk_sum[far].astype(jnp.bfloat16)
        dkv_ref[j, 1, 0] = dv_sum[near].astype(jnp.bfloat16)
        dkv_ref[j, 1, 1] = dv_sum[far].astype(jnp.bfloat16)


def attention_core(queries, kv_all, attn_cotangent, place):
    tok_rows, q_cols = queries.shape
    count, _, _, half_rows, kv_cols = kv_all.shape
    kv_heads = kv_cols // HD
    width = q_cols // kv_heads
    rows = width // HD * half_rows
    total = count * tok_rows
    wide = pl.BlockSpec((tok_rows, width), lambda g, place: (0, g))
    pair = pl.BlockSpec((count, 2, 2, half_rows, HD), lambda g, place: (0, 0, 0, 0, g))
    like_q = jax.ShapeDtypeStruct(queries.shape, jnp.bfloat16)
    flops = 7 * 2 * tok_rows * q_cols * total // 2
    return pl.pallas_call(
        attention_kernel,
        out_shape=(like_q, like_q, jax.ShapeDtypeStruct(kv_all.shape, jnp.bfloat16)),
        grid_spec=pltpu.PrefetchScalarGridSpec(
            num_scalar_prefetch=1,
            grid=(kv_heads,),
            in_specs=[wide, pair, wide],
            out_specs=(wide, wide, pair),
            scratch_shapes=[
                pltpu.VMEM((total, HD), jnp.bfloat16),
                pltpu.VMEM((total, HD), jnp.bfloat16),
                pltpu.VMEM((total, HD), jnp.float32),
                pltpu.VMEM((total, HD), jnp.float32),
                pltpu.VMEM((total, rows), jnp.float32),
                pltpu.VMEM((rows, HD), jnp.bfloat16),
                pltpu.VMEM((rows, HD), jnp.bfloat16),
                pltpu.VMEM((HD, rows), jnp.float32),
            ],
        ),
        compiler_params=pltpu.CompilerParams(vmem_limit_bytes=VMEM_BYTES),
        cost_estimate=pl.CostEstimate(
            flops=3 * flops, bytes_accessed=16 * 1024 * 1024, transcendentals=total * q_cols // 2
        ),
        name="attention_both",
    )(place.reshape(1).astype(jnp.int32), queries, kv_all, attn_cotangent)


def attention(queries, key_states, value_states, attn_cotangent):
    tok_rows = queries.shape[0]
    half_rows = tok_rows // 2
    kv_cols = key_states.shape[1]
    count = lax.axis_size("ctx")
    kv = jnp.stack([key_states, value_states])
    kv_all = lax.all_gather(kv, "ctx", axis=0).reshape(count, 2, 2, half_rows, kv_cols)
    attn_output, query_grad, dkv = attention_core(
        queries, kv_all, attn_cotangent, lax.axis_index("ctx")
    )
    mine = lax.psum_scatter(
        dkv.reshape(count, 2, tok_rows, kv_cols), "ctx", scatter_dimension=0, tiled=False
    )
    return (attn_output, query_grad, mine[0], mine[1])


def in_order(ref, step, steps):
    pieces = ref.shape[0]
    early = step < steps // 2
    return [ref[jnp.where(early, j, pieces - 1 - j)] for j in range(pieces)]


def put_in_order(ref, value, step, steps):
    pieces, rows = ref.shape[0], ref.shape[1]
    early = step < steps // 2
    for j in range(pieces):
        ref[jnp.where(early, j, pieces - 1 - j)] = value[j * rows : (j + 1) * rows].astype(
            ref.dtype
        )


def whole(ref, step, steps):
    return jnp.concatenate(in_order(ref, step, steps), axis=0)


def causal_decay(col, row, flip):
    shape = (col.shape[0], row.shape[1])
    down = lax.broadcasted_iota(jnp.int32, shape, 0)
    across = lax.broadcasted_iota(jnp.int32, shape, 1)
    if flip:
        return jnp.exp(jnp.where(across >= down, row - col, NEGATIVE))
    return jnp.exp(jnp.where(down >= across, col - row, NEGATIVE))


def forward_kernel(steps, x_ref, b_ref, c_ref, col_ref, row_ref, mixed_ref, state_ref, state):
    step = pl.program_id(0)

    @pl.when(step == 0)
    def _():
        state[...] = jnp.zeros_like(state)

    x = whole(x_ref, step, steps)
    b = whole(b_ref, step, steps)
    c = whole(c_ref, step, steps)
    col, row = col_ref[...], row_ref[0]
    last = col[CHUNK - 1 : CHUNK]
    weights = (causal_decay(col, row, False) * dot(c, b, 1, 1)).astype(jnp.bfloat16)
    entering = state[...]
    entering_short = entering.astype(jnp.bfloat16)
    state_ref[0] = entering_short
    mixed = dot(weights, x, 1, 0) + jnp.exp(col) * dot(c, entering_short, 1, 0)
    put_in_order(mixed_ref, mixed, step, steps)
    shrunk = (b.astype(jnp.float32) * jnp.exp(last - col)).astype(jnp.bfloat16)
    state[...] = jnp.exp(last) * entering + dot(shrunk, x, 0, 0)


def backward_kernel(
    steps, x_ref, dm_ref, b_ref, c_ref, col_ref, row_ref, state_ref,
    input_ref, maps_ref, adjoint,
):
    step = steps - 1 - pl.program_id(0)

    @pl.when(pl.program_id(0) == 0)
    def _():
        adjoint[...] = jnp.zeros_like(adjoint)

    x = whole(x_ref, step, steps)
    dm = whole(dm_ref, step, steps)
    b = whole(b_ref, step, steps)
    c = whole(c_ref, step, steps)
    col, row = col_ref[...], row_ref[0]
    last = col[CHUNK - 1 : CHUNK]
    shrink, grow = jnp.exp(last - col), jnp.exp(col)
    entering = adjoint[...]
    entering_short = entering.astype(jnp.bfloat16)
    decay_t = causal_decay(col, row, True)
    weights_t = (decay_t * dot(b, c, 1, 1)).astype(jnp.bfloat16)
    input_g = dot(weights_t, dm, 1, 0) + shrink * dot(b, entering_short, 1, 0)
    put_in_order(input_ref, input_g, step, steps)
    pairs_t = (decay_t * dot(x, dm, 1, 1)).astype(jnp.bfloat16)
    write_g = dot(pairs_t, c, 1, 0) + shrink * dot(x, entering_short, 1, 1)
    pairs = (causal_decay(col, row, False) * dot(dm, x, 1, 1)).astype(jnp.bfloat16)
    read_g = dot(pairs, b, 1, 0) + grow * dot(dm, state_ref[0], 1, 1)
    put_in_order(maps_ref, jnp.concatenate([write_g, read_g], axis=1), step, steps)
    grown = (c.astype(jnp.float32) * grow).astype(jnp.bfloat16)
    adjoint[...] = jnp.exp(last) * entering + dot(grown, dm, 0, 0)


def ssm_specs(count, half_rows, steps, order):
    per = CHUNK // half_rows

    def rows_spec(cols):
        def place(i):
            step = order(i)
            early = step < steps // 2
            return (
                jnp.where(early, step, steps - 1 - step), jnp.where(early, 0, 1), 0, 0
            )

        return pl.BlockSpec((per, pl.Squeezed(), half_rows, cols), place)

    return (
        rows_spec,
        pl.BlockSpec((CHUNK, 1), lambda i: (order(i), 0)),
        pl.BlockSpec((1, 1, CHUNK), lambda i: (order(i), 0, 0)),
    )


def scan_forward(x, b, c, col, row):
    count, _, half_rows, cols = x.shape
    states = b.shape[-1]
    steps = count * 2 * half_rows // CHUNK
    rows_spec, col_spec, row_spec = ssm_specs(count, half_rows, steps, lambda i: i)
    return pl.pallas_call(
        functools.partial(forward_kernel, steps),
        grid=(steps,),
        in_specs=[rows_spec(cols), rows_spec(states), rows_spec(states), col_spec, row_spec],
        out_specs=(rows_spec(cols), pl.BlockSpec((1, states, cols), lambda i: (i, 0, 0))),
        out_shape=(
            jax.ShapeDtypeStruct(x.shape, jnp.bfloat16),
            jax.ShapeDtypeStruct((steps, states, cols), jnp.bfloat16),
        ),
        scratch_shapes=[pltpu.VMEM((states, cols), jnp.float32)],
        compiler_params=pltpu.CompilerParams(vmem_limit_bytes=VMEM_BYTES),
        cost_estimate=pl.CostEstimate(
            flops=8 * 10**9, bytes_accessed=8 * 1024 * 1024, transcendentals=10**6
        ),
        name="scan_forward",
    )(x, b, c, col, row)


def scan_backward(x, dm, b, c, col, row, state):
    count, _, half_rows, cols = x.shape
    states = b.shape[-1]
    steps = count * 2 * half_rows // CHUNK
    rows_spec, col_spec, row_spec = ssm_specs(
        count, half_rows, steps, lambda i: steps - 1 - i
    )
    return pl.pallas_call(
        functools.partial(backward_kernel, steps),
        grid=(steps,),
        in_specs=[
            rows_spec(cols), rows_spec(cols), rows_spec(states), rows_spec(states),
            col_spec, row_spec,
            pl.BlockSpec((1, states, cols), lambda i: (steps - 1 - i, 0, 0)),
        ],
        out_specs=(rows_spec(cols), rows_spec(2 * states)),
        out_shape=(
            jax.ShapeDtypeStruct(x.shape, jnp.bfloat16),
            jax.ShapeDtypeStruct((count, 2, half_rows, 2 * states), jnp.bfloat16),
        ),
        scratch_shapes=[pltpu.VMEM((states, cols), jnp.float32)],
        compiler_params=pltpu.CompilerParams(vmem_limit_bytes=VMEM_BYTES),
        cost_estimate=pl.CostEstimate(
            flops=16 * 10**9, bytes_accessed=12 * 1024 * 1024, transcendentals=2 * 10**6
        ),
        name="scan_backward",
    )(x, dm, b, c, col, row, state)


def to_channels(values):
    return lax.all_to_all(values, "ctx", split_axis=1, concat_axis=0, tiled=True)


def to_tokens(values):
    return lax.all_to_all(values, "ctx", split_axis=0, concat_axis=1, tiled=True)


def ssm_layer(
    ssm_input, ssm_gate, state_write, state_read, log_decay, skip_gain, norm_gain, ssm_cotangent
):
    tok_rows, channel_count = ssm_input.shape
    head_count = log_decay.shape[1]
    half_rows = tok_rows // 2
    head_dim = channel_count // head_count
    count = lax.axis_size("ctx")
    own_cols = channel_count // count
    states = state_write.shape[1]
    folded = (count, 2, half_rows)
    x_all = to_channels(ssm_input).reshape(*folded, own_cols)
    b_all = lax.all_gather(state_write, "ctx", axis=0).reshape(*folded, states)
    c_all = lax.all_gather(state_read, "ctx", axis=0).reshape(*folded, states)
    decay_all = lax.all_gather(log_decay, "ctx", axis=0).reshape(*folded, head_count)
    head = lax.axis_index("ctx") * own_cols // head_dim
    own_decay = lax.dynamic_index_in_dim(decay_all, head, 3, False)
    ordered = jnp.concatenate([own_decay[:, 0], own_decay[::-1, 1]]).reshape(-1, CHUNK)
    upto = jnp.triu(jnp.ones((CHUNK, CHUNK), jnp.float32))
    log_total = jnp.dot(ordered, upto, precision=PRECISE)
    col = log_total.reshape(-1, 1)
    row = log_total[:, None, :]
    mixed_all, state_all = scan_forward(x_all, b_all, c_all, col, row)
    skip = jnp.repeat(skip_gain, head_dim)[None, :]
    mixed = to_tokens(mixed_all.reshape(count * tok_rows, own_cols)).astype(jnp.float32)
    mixed = mixed + skip * ssm_input.astype(jnp.float32)
    gate = ssm_gate.astype(jnp.float32)
    sigmoid = jax.nn.sigmoid(gate)
    gated = mixed * gate * sigmoid
    d_normed = ssm_cotangent.astype(jnp.float32) * norm_gain
    sums = lax.psum(
        jnp.stack([jnp.sum(gated * gated, axis=1), jnp.sum(d_normed * gated, axis=1)]), "tp"
    )
    root_mean = jnp.sqrt(sums[0] / CH + EPSILON)[:, None]
    inner_mean = (sums[1] / CH)[:, None] / root_mean
    normed = gated / root_mean
    ssm_output = (normed * norm_gain).astype(jnp.bfloat16)
    d_gated = (d_normed - normed * inner_mean) / root_mean
    d_mixed = d_gated * gate * sigmoid
    gate_grad = (d_gated * mixed * sigmoid * (1.0 + gate * (1.0 - sigmoid))).astype(jnp.bfloat16)
    dm_all = to_channels(d_mixed.astype(jnp.bfloat16)).reshape(*folded, own_cols)
    input_all, maps_all = scan_backward(x_all, dm_all, b_all, c_all, col, row, state_all)
    input_g = to_tokens(input_all.reshape(count * tok_rows, own_cols)).astype(jnp.float32)
    input_grad = (input_g + skip * d_mixed).astype(jnp.bfloat16)
    maps = lax.psum_scatter(
        maps_all.reshape(count, tok_rows, 2 * states), "ctx", scatter_dimension=0, tiled=False
    )
    maps = lax.psum(maps, "tp").astype(jnp.float32)
    return (ssm_output, input_grad, gate_grad, maps[:, :states], maps[:, states:])


def per_device(
    ssm_input,
    ssm_gate,
    state_write,
    state_read,
    log_decay,
    skip_gain,
    norm_gain,
    ssm_cotangent,
    queries,
    key_states,
    value_states,
    attn_cotangent,
):
    ssm_results = ssm_layer(
        ssm_input, ssm_gate, state_write, state_read, log_decay, skip_gain, norm_gain, ssm_cotangent
    )
    attn_results = attention(queries, key_states, value_states, attn_cotangent)
    return ssm_results + attn_results


def solution(mesh):
    placed = (
        P("ctx", "tp"),
        P("ctx", "tp"),
        P("ctx", None),
        P("ctx", None),
        P("ctx", "tp"),
        P("tp"),
        P("tp"),
        P("ctx", "tp"),
        P("ctx", "tp"),
        P("ctx", "tp"),
        P("ctx", "tp"),
        P("ctx", "tp"),
    )
    return jax.shard_map(
        per_device,
        mesh=mesh,
        in_specs=placed,
        out_specs=(
            P("ctx", "tp"),
            P("ctx", "tp"),
            P("ctx", "tp"),
            P("ctx", None),
            P("ctx", None),
            P("ctx", "tp"),
            P("ctx", "tp"),
            P("ctx", "tp"),
            P("ctx", "tp"),
        ),
        check_vma=False,
    )
```

time: 1350 us -> 542 us (0.40)
  waiting for transfers between devices: 866 us -> 225 us
  other arithmetic: 165 us -> 10.6 us
  matrix products: 110 us -> 0.29 us
  blocking collectives: 116 us -> 208 us
  Pallas kernels: 0 us -> 55.6 us
  local copies, waits for them, and re-layouts: 53.2 us -> 14.6 us
    all_gather x6 -> x1, waiting for transfers between devices: 624 us -> 76.1 us  [attention(): lax.all_gather(kv, 'ctx', axis=0).reshape(count, 2, 2, half_rows, kv_cols)]
    psum x3 -> x1, waiting for transfers between devices: 120 us -> 0.01 us  [ssm_layer(): maps = lax.psum(maps, 'tp').astype(jnp.float32)]
    dot_general x40 -> x1, matrix products: 110 us -> 0.29 us  [ssm_layer(): log_total = jnp.dot(ordered, upto, precision=PRECISE)]
    add x36 -> x1, other arithmetic: 107 us -> 0.01 us  [ssm_layer(): upto = jnp.triu(jnp.ones((CHUNK, CHUNK), jnp.float32))]
    all_to_all x0 -> x2, blocking collectives: none -> 73.5 us  [the longest x1 41.7 us: to_tokens(): lax.all_to_all(values, 'ctx', split_axis=0, concat_axis=1, tiled=True)]
    pallas_call x0 -> x3, Pallas kernels: none -> 55.6 us  [the longest x1 42.9 us: attention_core(): pl.pallas_call(attention_kernel, out_shape=(like_q, like_q, jax.ShapeDtyp...]
    all_gather x2 -> x3, blocking collectives: 111 us -> 132 us  [the longest x1 51.6 us: ssm_layer(): lax.all_gather(log_decay, 'ctx', axis=0).reshape(*folded, head_count)]
    all_to_all x0 -> x2, waiting for transfers between devices: none -> 15.5 us  [the longest x1 15.5 us: to_tokens(): lax.all_to_all(values, 'ctx', split_axis=0, concat_axis=1, tiled=True)]
  transfers between devices with their start and end apart: 11 -> 6, of which waited for: 11 -> 4; matrix products, arithmetic and copies ran while one was open for 23% -> 1% of each run, Pallas kernels for 0% -> 8%
where the time goes in v1:
time: 542 us; the launch traced here: 541 us
  waiting for transfers between devices  225 us (42%)
  blocking collectives  208 us (38%)
  Pallas kernels  55.6 us (10%)
  local copies, waits for them, and re-layouts  14.6 us (3%)
  between operations  14.1 us (3%)
  starting transfers between devices  12.4 us (2%)
  other arithmetic  10.6 us (2%)
    all_gather x1, waiting for transfers between devices, attention(): lax.all_gather(kv, 'ctx', axis=0).reshape(count, 2, 2, half_rows, kv_cols)  76.1 us
    reduce_scatter x1, waiting for transfers between devices, ssm_layer(): lax.psum_scatter(maps_all.reshape(count, tok_rows, 2 * states), 'ctx', sc...  75.5 us
    reduce_scatter x1, waiting for transfers between devices, attention(): lax.psum_scatter(dkv.reshape(count, 2, tok_rows, kv_cols), 'ctx', scatter...  57.9 us
    all_gather x1, blocking collectives, ssm_layer(): lax.all_gather(log_decay, 'ctx', axis=0).reshape(*folded, head_count)  51.6 us
    pallas_call x1, Pallas kernels, attention_core(): pl.pallas_call(attention_kernel, out_shape=(like_q, like_q, jax.ShapeDtyp...  42.9 us
    all_to_all x1, blocking collectives, to_tokens(): lax.all_to_all(values, 'ctx', split_axis=0, concat_axis=1, tiled=True)  41.7 us
    all_gather x1, blocking collectives, ssm_layer(): b_all = lax.all_gather(state_write, 'ctx', axis=0).reshape(*folded, states)  40.6 us
    all_gather x1, blocking collectives, ssm_layer(): c_all = lax.all_gather(state_read, 'ctx', axis=0).reshape(*folded, states)  39.8 us
  transfers between devices with their start and end apart: 6, of which 4 were waited for; matrix products, arithmetic and copies ran while one was open for 1% of the time, Pallas kernels for 8%

profile of v1, /device:TPU:0, one launch (start us, length us, event | category | flops | bytes accessed | tf_op | source)
XLA Modules:
  0.0 540.7 jit_solution(16232512402296992353)
XLA Ops:
  7.2 2.3 copy.57
  9.5 8.4 %all-to-all-start = ((bf16[128,16,256]{2,0,1:T(8,128)(2,1)}), bf16[128,16,256]{2,0,1:T(8,128)(2,1)S(1)}, u32[]{:S(2)}, u32[]{:S(2)}) async-start(bf16[128,16,256]{2,0,1:T(8,128)(2,1)} %bitcast.57), calls=%async_computation | async-start | bytes 2097152 | tf_op jit(solution)/shard_map/all_to_all | solution.py:315
  18.0 51.6 %all-gather.2 = f32[2048,16]{0,1:T(8,128)S(1)} all-gather(f32[128,16]{0,1:T(8,128)S(1)} %copy-done.18), channel_id=4, replica_groups=mesh['ctx'=16,'tp'=2] {'ctx'}, dimensions={0}, use_global_device_ids=true | all-gather | bytes 139264 | tf_op jit(solution)/shard_map/all_gather | solution.py:336
  70.3 0.4 copy.51
  70.7 40.6 %all-gather = bf16[2048,128]{1,0:T(8,128)(2,1)S(1)} all-gather(bf16[128,128]{1,0:T(8,128)(2,1)S(1)} %copy-done.16), channel_id=2, replica_groups=mesh['ctx'=16,'tp'=2] {'ctx'}, dimensions={0}, use_global_device_ids=true | all-gather | bytes 557056 | tf_op jit(solution)/shard_map/all_gather | solution.py:334
  111.3 39.8 %all-gather.1 = bf16[2048,128]{1,0:T(8,128)(2,1)S(1)} all-gather(bf16[128,128]{1,0:T(8,128)(2,1)S(1)} %copy-done.17), channel_id=3, replica_groups=mesh['ctx'=16,'tp'=2] {'ctx'}, dimensions={0}, use_global_device_ids=true | all-gather | bytes 557056 | tf_op jit(solution)/shard_map/all_gather | solution.py:335
  151.2 4.7 scan_forward.1
  155.9 0.8 copy-done.4
  156.7 3.8 all-to-all-start.1
  160.6 15.5 %all-to-all-done.1 = bf16[16,128,256]{2,1,0:T(8,128)(2,1)S(1)} async-done(((bf16[16,128,256]{2,1,0:T(8,128)(2,1)}), bf16[16,128,256]{2,1,0:T(8,128)(2,1)S(1)}, u32[]{:S(2)}, u32[]{:S(2)}) %all-to-all-start.1) | async-done | bytes 1048608 | tf_op jit(solution)/shard_map/all_to_all | solution.py:319
  176.6 1.0 copy-done.9
  177.6 1.0 copy-done.11
  178.7 0.3 copy-done.12
  179.0 2.4 multiply_reduce_fusion.1
  181.4 2.5 psum.14
  183.9 4.6 fusion.7
  188.5 0.8 fusion.15
  189.3 0.6 copy-done.6
  190.0 31.8 %all_to_all.58 = bf16[128,16,256]{2,0,1:T(8,128)(2,1)S(1)} all-to-all(bf16[128,16,256]{2,0,1:T(8,128)(2,1)S(1)} %bitcast.74), channel_id=1, replica_groups=mesh['ctx'=16,'tp'=2] {'ctx'}, dimensions={1} | all-to-all | bytes 2097152 | tf_op jit(solution)/shard_map/all_to_all | solution.py:315
  221.8 8.0 %scan_backward.1 = (bf16[16,2,64,256]{3,2,1,0:T(8,128)(2,1)S(1)}, bf16[16,2,64,256]{3,2,1,0:T(8,128)(2,1)}) custom-call(bf16[16,2,64,256]{3,2,1,0:T(8,128)(2,1)S(1)} %bitcast.60, bf16[16,2,64,256]{3,2,1,0:T(8,128)(2,1)S(1)} %bitcast.64, bf16[16,2,64,128]{3,2,1,0:T(8,128)(2,1)S(1)} %bitcast.66, bf16[16,2,64,128]{3,2,1,0:T(8,128)(2,1)S(1)} %bitcast.68, ...), custom_call_target="tpu_custom_call" | custom-call | flops 16000000000 | bytes 12582912 | tf_op jit(solution)/shard_map/scan_backward/pallas_call | solution.py:292
  229.9 0.7 pad_maximum_fusion
  230.7 75.5 %reduce-scatter.3.cloned.1.call-done = bf16[1,128,256]{2,1,0:T(8,128)(2,1)} async-done(((bf16[16,128,256]{2,1,0:T(8,128)(2,1)}), bf16[1,128,256]{2,1,0:T(8,128)(2,1)}) %reduce-scatter.3.cloned.1.call-update) | async-done | bytes 65552 | tf_op jit(solution)/shard_map/reduce_scatter | solution.py:366
  306.3 76.1 %all-gather.6.cloned.1.call-done = bf16[32,128,512]{2,1,0:T(8,128)(2,1)} async-done(((bf16[2,128,512]{2,1,0:T(8,128)(2,1)}), bf16[32,128,512]{2,1,0:T(8,128)(2,1)}) %all-gather.6.cloned.1.call-update) | async-done | bytes 4194320 | tf_op jit(solution)/shard_map/all_gather | solution.py:150
  382.4 1.2 copy-done.2
  383.6 1.2 copy-done.3
  384.9 42.9 %attention_both.1 = (bf16[128,4096]{1,0:T(8,128)(2,1)}, bf16[128,4096]{1,0:T(8,128)(2,1)}, bf16[16,2,2,64,512]{4,3,2,1,0:T(8,128)(2,1)}) custom-call(s32[1]{0:T(128)} %bitcast.20.place_ref, bf16[128,4096]{1,0:T(8,128)(2,1)S(1)} %copy-done.2, bf16[16,2,2,64,512]{4,3,2,1,0:T(8,128)(2,1)} %bitcast.88, bf16[128,4096]{1,0:T(8,128)(2,1)S(1)} %copy-done.3), custom_call_target="tpu_custom_call" | custom-call | flops 22548578304 | bytes 16777216 | tf_op jit(solution)/shard_map/attention_both/pallas_call | solution.py:117
  427.8 41.7 %all_to_all.59 = bf16[16,128,256]{2,1,0:T(8,128)(2,1)S(1)} all-to-all(bf16[16,128,256]{2,1,0:T(8,128)(2,1)S(1)} %bitcast.63), channel_id=1, replica_groups=mesh['ctx'=16,'tp'=2] {'ctx'}, dimensions={0} | all-to-all | bytes 2097152 | tf_op jit(solution)/shard_map/all_to_all | solution.py:319
  470.0 1.3 copy-done.7
  471.6 1.6 add_convert_fusion
  473.2 1.4 fusion.17
  474.6 57.9 %reduce-scatter.5.cloned.1.call-done = bf16[1,2,128,512]{3,2,1,0:T(8,128)(2,1)} async-done(((bf16[16,2,128,512]{3,2,1,0:T(8,128)(2,1)}), bf16[1,2,128,512]{3,2,1,0:T(8,128)(2,1)}) %reduce-scatter.5.cloned.1.call-update) | async-done | bytes 262160 | tf_op jit(solution)/shard_map/reduce_scatter | solution.py:154
  532.5 1.7 slice_bitcast_fusion
  (60 shorter events, 2.3 us)
Async XLA Ops:
  7.2 153.4 %copy-start = (f32[16]{0:T(128)S(1)}, f32[16]{0:T(128)}, u32[]{:S(2)}) copy-start(f32[16]{0:T(128)} %param.17) | copy-start | bytes 196
  7.2 10.8 %copy-start.18 = (f32[128,16]{0,1:T(8,128)S(1)}, f32[128,16]{0,1:T(8,128)}, u32[]{:S(2)}) copy-start(f32[128,16]{0,1:T(8,128)} %param.16) | copy-start | bytes 24580
  9.5 61.2 %copy-start.16 = (bf16[128,128]{1,0:T(8,128)(2,1)S(1)}, bf16[128,128]{1,0:T(8,128)(2,1)}, u32[]{:S(2)}) copy-start(bf16[128,128]{1,0:T(8,128)(2,1)} %param.14) | copy-start | bytes 98308
  9.5 101.8 %copy-start.17 = (bf16[128,128]{1,0:T(8,128)(2,1)S(1)}, bf16[128,128]{1,0:T(8,128)(2,1)}, u32[]{:S(2)}) copy-start(bf16[128,128]{1,0:T(8,128)(2,1)} %param.15) | copy-start | bytes 98308
  9.5 141.7 %all-to-all-start = ((bf16[128,16,256]{2,0,1:T(8,128)(2,1)}), bf16[128,16,256]{2,0,1:T(8,128)(2,1)S(1)}, u32[]{:S(2)}, u32[]{:S(2)}) async-start(bf16[128,16,256]{2,0,1:T(8,128)(2,1)} %bitcast.57), calls=%async_computation | async-start | bytes 2097152 | tf_op jit(solution)/shard_map/all_to_all | solution.py:315
  70.7 85.2 %copy-start.1 = (f32[1,2048]{0,1:T(8,128)}, f32[1,2048]{0,1:T(8,128)S(1)}, u32[]{:S(2)}) copy-start(f32[1,2048]{0,1:T(8,128)S(1)} %copy.51) | copy-start | bytes 24580
  155.9 0.8 copy-start.4
  156.7 19.5 %all-to-all-start.1 = ((bf16[16,128,256]{2,1,0:T(8,128)(2,1)}), bf16[16,128,256]{2,1,0:T(8,128)(2,1)S(1)}, u32[]{:S(2)}, u32[]{:S(2)}) async-start(bf16[16,128,256]{2,1,0:T(8,128)(2,1)} %bitcast.7), calls=%async_computation.1 | async-start | bytes 2097152 | tf_op jit(solution)/shard_map/all_to_all | solution.py:319
  160.5 145.7 %reduce-scatter.3.cloned.1.call-start = ((), (), s32[]{:S(2)}) async-start(), calls=%async_computation.6 | async-start | bytes 1114112 | tf_op jit(solution)/shard_map/reduce_scatter | solution.py:366
  176.4 1.3 copy-start.9
  176.4 2.3 copy-start.11
  176.4 2.6 copy-start.12
  176.4 2.6 copy-start.15
  176.6 4.8 copy-start.8
  188.5 1.4 copy-start.6
  189.9 31.9 %copy-start.5 = (bf16[8,128,256]{2,1,0:T(8,128)(2,1)S(1)}, bf16[8,128,256]{2,1,0:T(8,128)(2,1)}, u32[]{:S(2)}) copy-start(bf16[8,128,256]{2,1,0:T(8,128)(2,1)} %copy-done.4) | copy-start | bytes 1572868
  221.8 8.1 %copy-start.13 = (bf16[128,512]{1,0:T(8,128)(2,1)S(1)}, bf16[128,512]{1,0:T(8,128)(2,1)}, u32[]{:S(2)}) copy-start(bf16[128,512]{1,0:T(8,128)(2,1)} %param.22) | copy-start | bytes 393220
  221.8 8.1 %copy-start.14 = (bf16[128,512]{1,0:T(8,128)(2,1)S(1)}, bf16[128,512]{1,0:T(8,128)(2,1)}, u32[]{:S(2)}) copy-start(bf16[128,512]{1,0:T(8,128)(2,1)} %param.21) | copy-start | bytes 393220
  229.8 152.6 %all-gather.6.cloned.1.call-start = ((), (), s32[]{:S(2)}) async-start(), calls=%async_computation.9 | async-start | bytes 4456448 | tf_op jit(solution)/shard_map/all_gather | solution.py:150
  230.7 242.5 %all-reduce.2.cloned.1.call-start = ((), (), s32[]{:S(2)}) async-start(), calls=%async_computation.7 | async-start | bytes 131072 | tf_op jit(solution)/shard_map/psum | solution.py:369
  306.2 226.3 %reduce-scatter.5.cloned.1.call-start = ((), (), s32[]{:S(2)}) async-start(), calls=%async_computation.8 | async-start | bytes 4456448 | tf_op jit(solution)/shard_map/reduce_scatter | solution.py:154
  382.4 1.2 copy-start.2
  383.6 1.2 copy-start.3
  469.7 1.6 copy-start.7
  469.7 1.8 copy-start.10
Sparse Core Ops, SparseCore 0:
  230.0 76.2 reduce-scatter.2
  309.9 72.4 all-gather.5
  384.8 16.3 all-reduce.1
  427.9 104.5 reduce-scatter.4

commit v2 on v1

--- a/solution.py
+++ b/solution.py
@@ -141,20 +141,20 @@
     )(place.reshape(1).astype(jnp.int32), queries, kv_all, attn_cotangent)
 
 
-def attention(queries, key_states, value_states, attn_cotangent):
-    tok_rows = queries.shape[0]
-    half_rows = tok_rows // 2
-    kv_cols = key_states.shape[1]
-    count = lax.axis_size("ctx")
+def gather_pair(key_states, value_states):
+    tok_rows, kv_cols = key_states.shape
     kv = jnp.stack([key_states, value_states])
-    kv_all = lax.all_gather(kv, "ctx", axis=0).reshape(count, 2, 2, half_rows, kv_cols)
-    attn_output, query_grad, dkv = attention_core(
-        queries, kv_all, attn_cotangent, lax.axis_index("ctx")
-    )
+    return lax.all_gather(kv, "ctx", axis=0).reshape(
+        lax.axis_size("ctx"), 2, 2, tok_rows // 2, kv_cols
+    )
+
+
+def scatter_pair(dkv):
+    count, _, _, half_rows, kv_cols = dkv.shape
     mine = lax.psum_scatter(
-        dkv.reshape(count, 2, tok_rows, kv_cols), "ctx", scatter_dimension=0, tiled=False
-    )
-    return (attn_output, query_grad, mine[0], mine[1])
+        dkv.reshape(count, 2, 2 * half_rows, kv_cols), "ctx", scatter_dimension=0, tiled=False
+    )
+    return (mine[0], mine[1])
 
 
 def in_order(ref, step, steps):
@@ -209,7 +209,7 @@
 
 def backward_kernel(
     steps, x_ref, dm_ref, b_ref, c_ref, col_ref, row_ref, state_ref,
-    input_ref, maps_ref, adjoint,
+    input_ref, write_ref, read_ref, adjoint,
 ):
     step = steps - 1 - pl.program_id(0)
 
@@ -234,7 +234,8 @@
     write_g = dot(pairs_t, c, 1, 0) + shrink * dot(x, entering_short, 1, 1)
     pairs = (causal_decay(col, row, False) * dot(dm, x, 1, 1)).astype(jnp.bfloat16)
     read_g = dot(pairs, b, 1, 0) + grow * dot(dm, state_ref[0], 1, 1)
-    put_in_order(maps_ref, jnp.concatenate([write_g, read_g], axis=1), step, steps)
+    put_in_order(write_ref, write_g, step, steps)
+    put_in_order(read_ref, read_g, step, steps)
     grown = (c.astype(jnp.float32) * grow).astype(jnp.bfloat16)
     adjoint[...] = jnp.exp(last) * entering + dot(grown, dm, 0, 0)
 
@@ -297,10 +298,11 @@
             col_spec, row_spec,
             pl.BlockSpec((1, states, cols), lambda i: (steps - 1 - i, 0, 0)),
         ],
-        out_specs=(rows_spec(cols), rows_spec(2 * states)),
+        out_specs=(rows_spec(cols), rows_spec(states), rows_spec(states)),
         out_shape=(
             jax.ShapeDtypeStruct(x.shape, jnp.bfloat16),
-            jax.ShapeDtypeStruct((count, 2, half_rows, 2 * states), jnp.bfloat16),
+            jax.ShapeDtypeStruct(b.shape, jnp.bfloat16),
+            jax.ShapeDtypeStruct(b.shape, jnp.bfloat16),
         ),
         scratch_shapes=[pltpu.VMEM((states, cols), jnp.float32)],
         compiler_params=pltpu.CompilerParams(vmem_limit_bytes=VMEM_BYTES),
@@ -311,16 +313,31 @@
     )(x, dm, b, c, col, row, state)
 
 
-def to_channels(values):
-    return lax.all_to_all(values, "ctx", split_axis=1, concat_axis=0, tiled=True)
-
-
-def to_tokens(values):
-    return lax.all_to_all(values, "ctx", split_axis=0, concat_axis=1, tiled=True)
-
-
-def ssm_layer(
-    ssm_input, ssm_gate, state_write, state_read, log_decay, skip_gain, norm_gain, ssm_cotangent
+def to_channels(values, extra=None):
+    count = lax.axis_size("ctx")
+    parts = values.reshape(values.shape[0], count, -1)
+    if extra is not None:
+        shape = (values.shape[0], count, extra.shape[1])
+        parts = jnp.concatenate([parts, jnp.broadcast_to(extra[:, None, :], shape)], axis=2)
+    blocks = jnp.transpose(parts, (1, 0, 2))
+    return lax.all_to_all(blocks, "ctx", split_axis=0, concat_axis=0)
+
+
+def to_owners(blocks):
+    return lax.all_to_all(blocks, "ctx", split_axis=0, concat_axis=0)
+
+
+def side_by_side(blocks):
+    return jnp.transpose(blocks, (1, 0, 2)).reshape(blocks.shape[1], -1)
+
+
+def from_other_core(values):
+    return lax.ppermute(values, "tp", [(0, 1), (1, 0)])
+
+
+def both_layers(
+    ssm_input, ssm_gate, state_write, state_read, log_decay, skip_gain, norm_gain, ssm_cotangent,
+    queries, key_states, value_states, attn_cotangent,
 ):
     tok_rows, channel_count = ssm_input.shape
     head_count = log_decay.shape[1]
@@ -330,12 +347,22 @@
     own_cols = channel_count // count
     states = state_write.shape[1]
     folded = (count, 2, half_rows)
-    x_all = to_channels(ssm_input).reshape(*folded, own_cols)
-    b_all = lax.all_gather(state_write, "ctx", axis=0).reshape(*folded, states)
-    c_all = lax.all_gather(state_read, "ctx", axis=0).reshape(*folded, states)
-    decay_all = lax.all_gather(log_decay, "ctx", axis=0).reshape(*folded, head_count)
-    head = lax.axis_index("ctx") * own_cols // head_dim
-    own_decay = lax.dynamic_index_in_dim(decay_all, head, 3, False)
+    share_maps = lax.axis_size("tp") == 2
+    kv_all = gather_pair(key_states, value_states)
+    if share_maps:
+        first = lax.axis_index("tp") == 0
+        arrived = to_channels(ssm_input, jnp.where(first, state_write, state_read))
+        own_map = arrived[:, :, own_cols:]
+        other_map = from_other_core(own_map)
+        b_all = jnp.where(first, own_map, other_map).reshape(*folded, states)
+        c_all = jnp.where(first, other_map, own_map).reshape(*folded, states)
+    else:
+        arrived = to_channels(ssm_input, jnp.concatenate([state_write, state_read], axis=1))
+        b_all = arrived[:, :, own_cols : own_cols + states].reshape(*folded, states)
+        c_all = arrived[:, :, own_cols + states :].reshape(*folded, states)
+    x_all = arrived[:, :, :own_cols].reshape(*folded, own_cols)
+    decay_rows = jnp.repeat(log_decay.T, head_dim // own_cols, axis=0)
+    own_decay = to_owners(decay_rows[:, None, :]).reshape(*folded)
     ordered = jnp.concatenate([own_decay[:, 0], own_decay[::-1, 1]]).reshape(-1, CHUNK)
     upto = jnp.triu(jnp.ones((CHUNK, CHUNK), jnp.float32))
     log_total = jnp.dot(ordered, upto, precision=PRECISE)
@@ -343,8 +370,8 @@
     row = log_total[:, None, :]
     mixed_all, state_all = scan_forward(x_all, b_all, c_all, col, row)
     skip = jnp.repeat(skip_gain, head_dim)[None, :]
-    mixed = to_tokens(mixed_all.reshape(count * tok_rows, own_cols)).astype(jnp.float32)
-    mixed = mixed + skip * ssm_input.astype(jnp.float32)
+    mixed = side_by_side(to_owners(mixed_all.reshape(count, tok_rows, own_cols)))
+    mixed = mixed.astype(jnp.float32) + skip * ssm_input.astype(jnp.float32)
     gate = ssm_gate.astype(jnp.float32)
     sigmoid = jax.nn.sigmoid(gate)
     gated = mixed * gate * sigmoid
@@ -359,36 +386,39 @@
     d_gated = (d_normed - normed * inner_mean) / root_mean
     d_mixed = d_gated * gate * sigmoid
     gate_grad = (d_gated * mixed * sigmoid * (1.0 + gate * (1.0 - sigmoid))).astype(jnp.bfloat16)
-    dm_all = to_channels(d_mixed.astype(jnp.bfloat16)).reshape(*folded, own_cols)
-    input_all, maps_all = scan_backward(x_all, dm_all, b_all, c_all, col, row, state_all)
-    input_g = to_tokens(input_all.reshape(count * tok_rows, own_cols)).astype(jnp.float32)
+    d_mixed_short, kv_all = lax.optimization_barrier((d_mixed.astype(jnp.bfloat16), kv_all))
+    attn_output, query_grad, dkv = attention_core(
+        queries, kv_all, attn_cotangent, lax.axis_index("ctx")
+    )
+    dm_all = to_channels(d_mixed_short).reshape(*folded, own_cols)
+    dkv, dm_all = lax.optimization_barrier((dkv, dm_all))
+    key_grad, value_grad = scatter_pair(dkv)
+    input_all, write_all, read_all = scan_backward(
+        x_all, dm_all, b_all, c_all, col, row, state_all
+    )
+    blocks = (count, tok_rows)
+    input_all = input_all.reshape(*blocks, own_cols)
+    write_all, read_all = write_all.reshape(*blocks, states), read_all.reshape(*blocks, states)
+    if share_maps:
+        kept = jnp.where(first, write_all, read_all)
+        passed = from_other_core(jnp.where(first, read_all, write_all))
+        maps_all = (kept.astype(jnp.float32) + passed.astype(jnp.float32)).astype(jnp.bfloat16)
+    else:
+        maps_all = jnp.concatenate([write_all, read_all], axis=2)
+    back = to_owners(jnp.concatenate([input_all, maps_all], axis=2))
+    input_g = side_by_side(back[:, :, :own_cols]).astype(jnp.float32)
     input_grad = (input_g + skip * d_mixed).astype(jnp.bfloat16)
-    maps = lax.psum_scatter(
-        maps_all.reshape(count, tok_rows, 2 * states), "ctx", scatter_dimension=0, tiled=False
-    )
-    maps = lax.psum(maps, "tp").astype(jnp.float32)
-    return (ssm_output, input_grad, gate_grad, maps[:, :states], maps[:, states:])
-
-
-def per_device(
-    ssm_input,
-    ssm_gate,
-    state_write,
-    state_read,
-    log_decay,
-    skip_gain,
-    norm_gain,
-    ssm_cotangent,
-    queries,
-    key_states,
-    value_states,
-    attn_cotangent,
-):
-    ssm_results = ssm_layer(
-        ssm_input, ssm_gate, state_write, state_read, log_decay, skip_gain, norm_gain, ssm_cotangent
-    )
-    attn_results = attention(queries, key_states, value_states, attn_cotangent)
-    return ssm_results + attn_results
+    maps = jnp.sum(back[:, :, own_cols:].astype(jnp.float32), axis=0)
+    if share_maps:
+        other = from_other_core(maps)
+        write_grad, read_grad = jnp.where(first, maps, other), jnp.where(first, other, maps)
+    else:
+        maps = lax.psum(maps.astype(jnp.bfloat16), "tp").astype(jnp.float32)
+        write_grad, read_grad = maps[:, :states], maps[:, states:]
+    return (
+        ssm_output, input_grad, gate_grad, write_grad, read_grad,
+        attn_output, query_grad, key_grad, value_grad,
+    )
 
 
 def solution(mesh):
@@ -407,7 +437,7 @@
         P("ctx", "tp"),
     )
     return jax.shard_map(
-        per_device,
+        both_layers,
         mesh=mesh,
         in_specs=placed,
         out_specs=(

time: 542 us -> 326 us (0.60)
  blocking collectives: 208 us -> 62.4 us
  waiting for transfers between devices: 225 us -> 121 us
  starting transfers between devices: 12.4 us -> 36.9 us
    all_gather x3 -> x0, blocking collectives: 132 us -> none  [the longest x1 51.6 us: ssm_layer(): lax.all_gather(log_decay, 'ctx', axis=0).reshape(*folded, head_count)]
    reduce_scatter x2 -> x1, waiting for transfers between devices: 133 us -> 38.3 us  [scatter_pair(): lax.psum_scatter(dkv.reshape(count, 2, 2 * half_rows, kv_cols), 'ctx', sc...]
    all_gather x1, waiting for transfers between devices: 76.1 us -> 0.01 us  [gather_pair(): lax.all_gather(kv, 'ctx', axis=0)]
    all_to_all x2 -> x4, waiting for transfers between devices: 15.5 us -> 80.4 us  [the longest x2 43.6 us: to_owners(): return lax.all_to_all(blocks, 'ctx', split_axis=0, concat_axis=0)]
    all_to_all x2 -> x4, starting transfers between devices: 12.3 us -> 36.6 us  [the longest x2 20.3 us: to_owners(): return lax.all_to_all(blocks, 'ctx', split_axis=0, concat_axis=0)]
    all_to_all x2 -> x1, blocking collectives: 73.5 us -> 59.9 us  [to_owners(): return lax.all_to_all(blocks, 'ctx', split_axis=0, concat_axis=0)]
  transfers between devices with their start and end apart: 6 -> 9, of which waited for: 4 -> 5; matrix products, arithmetic and copies ran while one was open for 1% -> 6% of each run, Pallas kernels for 8% -> 17%
where the time goes in v2:
time: 326 us; the launch traced here: 325 us
  waiting for transfers between devices  121 us (37%)
  blocking collectives  62.4 us (19%)
  Pallas kernels  55 us (17%)
  starting transfers between devices  36.9 us (11%)
  local copies, waits for them, and re-layouts  19.3 us (6%)
  other arithmetic  16 us (5%)
  between operations  14.5 us (4%)
    all_to_all x1, blocking collectives, to_owners(): return lax.all_to_all(blocks, 'ctx', split_axis=0, concat_axis=0)  59.9 us
    all_to_all x2, waiting for transfers between devices, to_owners(): return lax.all_to_all(blocks, 'ctx', split_axis=0, concat_axis=0)  43.6 us
    pallas_call x1, Pallas kernels, attention_core(): pl.pallas_call(attention_kernel, out_shape=(like_q, like_q, jax.ShapeDtyp...  42.9 us
    reduce_scatter x1, waiting for transfers between devices, scatter_pair(): lax.psum_scatter(dkv.reshape(count, 2, 2 * half_rows, kv_cols), 'ctx', sc...  38.3 us
    all_to_all x2, waiting for transfers between devices, to_channels(): return lax.all_to_all(blocks, 'ctx', split_axis=0, concat_axis=0)  36.8 us
    all_to_all x2, starting transfers between devices, to_owners(): return lax.all_to_all(blocks, 'ctx', split_axis=0, concat_axis=0)  20.3 us
    all_to_all x2, starting transfers between devices, to_channels(): return lax.all_to_all(blocks, 'ctx', split_axis=0, concat_axis=0)  16.3 us
    unnamed x42, local copies, waits for them, and re-layouts  11 us
  transfers between devices with their start and end apart: 9, of which 5 were waited for; matrix products, arithmetic and copies ran while one was open for 6% of the time, Pallas kernels for 17%

profile of v2, /device:TPU:0, one launch (start us, length us, event | category | flops | bytes accessed | tf_op | source)
XLA Modules:
  0.0 325.0 jit_solution(9437002704753384931)
XLA Ops:
  7.2 8.5 %all-to-all-start.1 = ((f32[16,1,128]{2,1,0:T(1,128)}), f32[16,1,128]{2,1,0:T(1,128)S(1)}, u32[]{:S(2)}, u32[]{:S(2)}) async-start(f32[16,1,128]{2,1,0:T(1,128)} %bitcast.89), calls=%async_computation.1 | async-start | bytes 16384 | tf_op jit(solution)/shard_map/all_to_all | solution.py:327
  15.7 1.3 copy.51
  17.2 1.4 maximum_bitcast_fusion
  18.5 4.4 %all-to-all-done.1 = f32[16,1,128]{2,1,0:T(1,128)S(1)} async-done(((f32[16,1,128]{2,1,0:T(1,128)}), f32[16,1,128]{2,1,0:T(1,128)S(1)}, u32[]{:S(2)}, u32[]{:S(2)}) %all-to-all-start.1) | async-done | bytes 8224 | tf_op jit(solution)/shard_map/all_to_all | solution.py:327
  22.9 3.7 %all-to-all-start = ((bf16[16,128,384]{2,1,0:T(8,128)(2,1)}), bf16[16,128,384]{2,1,0:T(8,128)(2,1)S(1)}, u32[]{:S(2)}, u32[]{:S(2)}) async-start(bf16[16,128,384]{2,1,0:T(8,128)(2,1)} %maximum_bitcast_fusion), calls=%async_computation | async-start | bytes 3145728 | tf_op jit(solution)/shard_map/all_to_all | solution.py:323
  28.7 36.8 %all-to-all-done = bf16[16,128,384]{2,1,0:T(8,128)(2,1)S(1)} async-done(((bf16[16,128,384]{2,1,0:T(8,128)(2,1)}), bf16[16,128,384]{2,1,0:T(8,128)(2,1)S(1)}, u32[]{:S(2)}, u32[]{:S(2)}) %all-to-all-start) | async-done | bytes 1572896 | tf_op jit(solution)/shard_map/all_to_all | solution.py:323
  65.7 0.9 copy-done.12
  67.3 1.7 slice.42
  69.0 1.3 broadcast_select_fusion.2
  70.3 4.7 %scan_forward.1 = (bf16[16,2,64,256]{3,2,1,0:T(8,128)(2,1)}, bf16[8,128,256]{2,1,0:T(8,128)(2,1)S(1)}) custom-call(bf16[16,2,64,256]{3,2,1,0:T(8,128)(2,1)S(1)} %bitcast.64, bf16[16,2,64,128]{3,2,1,0:T(8,128)(2,1)S(1)} %bitcast.69, bf16[16,2,64,128]{3,2,1,0:T(8,128)(2,1)S(1)} %bitcast.67, f32[2048,1]{1,0:T(8,128)S(1)} %bitcast.62, ...), custom_call_target="tpu_custom_call" | custom-call | flops 8000000000 | bytes 8388608 | tf_op jit(solution)/shard_map/scan_forward/pallas_call | solution.py:268
  75.8 11.8 %all-to-all-start.2 = ((bf16[16,128,256]{2,1,0:T(8,128)(2,1)}), bf16[16,128,256]{2,1,0:T(8,128)(2,1)S(1)}, u32[]{:S(2)}, u32[]{:S(2)}) async-start(bf16[16,128,256]{2,1,0:T(8,128)(2,1)} %bitcast.8), calls=%async_computation.2 | async-start | bytes 2097152 | tf_op jit(solution)/shard_map/all_to_all | solution.py:327
  87.8 39.3 %all-to-all-done.2 = bf16[16,128,256]{2,1,0:T(8,128)(2,1)S(1)} async-done(((bf16[16,128,256]{2,1,0:T(8,128)(2,1)}), bf16[16,128,256]{2,1,0:T(8,128)(2,1)S(1)}, u32[]{:S(2)}, u32[]{:S(2)}) %all-to-all-start.2) | async-done | bytes 1048608 | tf_op jit(solution)/shard_map/all_to_all | solution.py:327
  127.6 1.0 copy-done.9
  128.6 1.0 copy-done.11
  129.9 2.5 multiply_reduce_fusion.1
  132.5 2.5 psum.7
  135.0 4.6 %fusion.7 = (bf16[128,4096]{1,0:T(8,128)(2,1)}, f32[128,4096]{1,0:T(8,128)S(1)}, bf16[128,4096]{1,0:T(8,128)(2,1)}) fusion(bf16[128,4096]{1,0:T(8,128)(2,1)S(1)} %copy-done.9, f32[128,4096]{1,0:T(8,128)} %bitcast.72, bf16[128,4096]{1,0:T(8,128)(2,1)} %param.12, f32[4096]{0:T(1024)S(1)} %bitcast.81, f32[128]{0:T(128)S(1)} %get-tuple-element.49, ...), kind=kLoop, calls=%fused_computation.11 | loop fusion | flops 11534336 | bytes 11568128 | tf_op jit(solution)/shard_map/convert_element_type | solution.py:388
  139.5 1.4 copy-done.6
  140.9 1.5 fusion.16
  142.4 2.3 copy.50
  144.7 12.6 %all-to-all-start.3 = ((bf16[16,128,256]{2,1,0:T(8,128)(2,1)}), bf16[16,128,256]{2,1,0:T(8,128)(2,1)S(1)}, u32[]{:S(2)}, u32[]{:S(2)}) async-start(bf16[16,128,256]{2,1,0:T(8,128)(2,1)} %bitcast.77), calls=%async_computation.3 | async-start | bytes 2097152 | tf_op jit(solution)/shard_map/all_to_all | solution.py:323
  157.4 1.2 copy-done.2
  158.7 1.2 copy-done.3
  159.9 42.9 %attention_both.1 = (bf16[128,4096]{1,0:T(8,128)(2,1)}, bf16[128,4096]{1,0:T(8,128)(2,1)}, bf16[16,2,2,64,512]{4,3,2,1,0:T(8,128)(2,1)}) custom-call(s32[1]{0:T(128)} %bitcast.13.place_ref, bf16[128,4096]{1,0:T(8,128)(2,1)S(1)} %copy-done.2, bf16[16,2,2,64,512]{4,3,2,1,0:T(8,128)(2,1)} %bitcast.92, bf16[128,4096]{1,0:T(8,128)(2,1)S(1)} %copy-done.3), custom_call_target="tpu_custom_call" | custom-call | flops 22548578304 | bytes 16777216 | tf_op jit(solution)/shard_map/attention_both/pallas_call | solution.py:117
  202.9 1.0 copy-done.5
  203.9 7.4 %scan_backward.1 = (bf16[16,2,64,256]{3,2,1,0:T(8,128)(2,1)S(1)}, bf16[16,2,64,128]{3,2,1,0:T(8,128)(2,1)S(1)}, bf16[16,2,64,128]{3,2,1,0:T(8,128)(2,1)S(1)}) custom-call(bf16[16,2,64,256]{3,2,1,0:T(8,128)(2,1)S(1)} %bitcast.65, bf16[16,2,64,256]{3,2,1,0:T(8,128)(2,1)S(1)} %bitcast.66, bf16[16,2,64,128]{3,2,1,0:T(8,128)(2,1)S(1)} %bitcast.70, ...), custom_call_target="tpu_custom_call" | custom-call | flops 16000000000 | bytes 12582912 | tf_op jit(solution)/shard_map/scan_backward/pallas_call | solution.py:293
  211.4 1.9 collective-permute-done.1
  213.8 59.9 %all_to_all.25 = bf16[16,128,384]{2,1,0:T(8,128)(2,1)S(1)} all-to-all(bf16[16,128,384]{2,1,0:T(8,128)(2,1)S(1)} %pad_maximum_fusion), channel_id=1, replica_groups=mesh['ctx'=16,'tp'=2] {'ctx'}, dimensions={0} | all-to-all | bytes 3145728 | tf_op jit(solution)/shard_map/all_to_all | solution.py:327
  274.3 1.4 copy-done.7
  275.9 1.6 add_convert_fusion
  278.2 38.3 %reduce-scatter.2.cloned.1.call-done = bf16[1,2,128,512]{3,2,1,0:T(8,128)(2,1)} async-done(((bf16[16,2,128,512]{3,2,1,0:T(8,128)(2,1)}), bf16[1,2,128,512]{3,2,1,0:T(8,128)(2,1)}) %reduce-scatter.2.cloned.1.call-update) | async-done | bytes 262160 | tf_op jit(solution)/shard_map/reduce_scatter | solution.py:154
  316.5 1.7 slice_bitcast_fusion
  (70 shorter events, 6.9 us)
Async XLA Ops:
  7.2 80.5 %copy-start = (f32[16]{0:T(128)S(1)}, f32[16]{0:T(128)}, u32[]{:S(2)}) copy-start(f32[16]{0:T(128)} %param.17) | copy-start | bytes 196
  7.2 9.8 %copy-start.18 = (bf16[128,128]{1,0:T(8,128)(2,1)S(1)}, bf16[128,128]{1,0:T(8,128)(2,1)}, u32[]{:S(2)}) copy-start(bf16[128,128]{1,0:T(8,128)(2,1)} %param.15) | copy-start | bytes 98308
  7.2 9.8 %copy-start.17 = (bf16[128,128]{1,0:T(8,128)(2,1)S(1)}, bf16[128,128]{1,0:T(8,128)(2,1)}, u32[]{:S(2)}) copy-start(bf16[128,128]{1,0:T(8,128)(2,1)} %param.14) | copy-start | bytes 98308
  7.2 15.7 %all-to-all-start.1 = ((f32[16,1,128]{2,1,0:T(1,128)}), f32[16,1,128]{2,1,0:T(1,128)S(1)}, u32[]{:S(2)}, u32[]{:S(2)}) async-start(f32[16,1,128]{2,1,0:T(1,128)} %bitcast.89), calls=%async_computation.1 | async-start | bytes 16384 | tf_op jit(solution)/shard_map/all_to_all | solution.py:327
  18.5 8.1 %copy-start.14 = (bf16[128,512]{1,0:T(8,128)(2,1)S(1)}, bf16[128,512]{1,0:T(8,128)(2,1)}, u32[]{:S(2)}) copy-start(bf16[128,512]{1,0:T(8,128)(2,1)} %param.22) | copy-start | bytes 393220
  18.5 8.1 %copy-start.15 = (bf16[128,512]{1,0:T(8,128)(2,1)S(1)}, bf16[128,512]{1,0:T(8,128)(2,1)}, u32[]{:S(2)}) copy-start(bf16[128,512]{1,0:T(8,128)(2,1)} %param.21) | copy-start | bytes 393220
  22.9 42.6 %all-to-all-start = ((bf16[16,128,384]{2,1,0:T(8,128)(2,1)}), bf16[16,128,384]{2,1,0:T(8,128)(2,1)S(1)}, u32[]{:S(2)}, u32[]{:S(2)}) async-start(bf16[16,128,384]{2,1,0:T(8,128)(2,1)} %maximum_bitcast_fusion), calls=%async_computation | async-start | bytes 3145728 | tf_op jit(solution)/shard_map/all_to_all | solution.py:323
  26.6 115.8 %all-gather.3.cloned.1.call-start = ((), (), s32[]{:S(2)}) async-start(), calls=%async_computation.7 | async-start | bytes 4456448 | tf_op jit(solution)/shard_map/all_gather | solution.py:147
  65.4 1.2 copy-start.12
  65.5 3.5 %collective-permute-start = (bf16[16,128,128]{2,1,0:T(8,128)(2,1)S(1)}, bf16[16,128,128]{2,1,0:T(8,128)(2,1)}, u32[]{:S(2)}, u32[]{:S(2)}) collective-permute-start(bf16[16,128,128]{2,1,0:T(8,128)(2,1)S(1)} %slice.43), channel_id=1, source_target_pairs={{0,1},{1,0},{2,3},{3,2},{4,5},{5,4},{6,7},{7,6},{8,9},{9,8},{10,11... | collective-permute-start | bytes 1572872 | tf_op jit(solution)/shard_map/ppermute | solution.py:335
  67.3 3.0 copy-start.1
  75.0 0.8 copy-start.4
  75.8 51.2 %all-to-all-start.2 = ((bf16[16,128,256]{2,1,0:T(8,128)(2,1)}), bf16[16,128,256]{2,1,0:T(8,128)(2,1)S(1)}, u32[]{:S(2)}, u32[]{:S(2)}) async-start(bf16[16,128,256]{2,1,0:T(8,128)(2,1)} %bitcast.8), calls=%async_computation.2 | async-start | bytes 2097152 | tf_op jit(solution)/shard_map/all_to_all | solution.py:327
  127.3 1.3 copy-start.9
  127.3 2.3 copy-start.11
  127.3 2.6 copy-start.13
  127.3 2.6 copy-start.16
  127.6 4.9 %copy-start.8 = (f32[16,16,8,256]{3,2,0,1:T(8,128)}, f32[16,16,8,256]{3,2,0,1:T(8,128)S(1)}, u32[]{:S(2)}) copy-start(f32[16,16,8,256]{3,2,0,1:T(8,128)S(1)} %copy.43) | copy-start | bytes 6291460
  139.5 1.4 copy-start.6
  144.7 58.1 %all-to-all-start.3 = ((bf16[16,128,256]{2,1,0:T(8,128)(2,1)}), bf16[16,128,256]{2,1,0:T(8,128)(2,1)S(1)}, u32[]{:S(2)}, u32[]{:S(2)}) async-start(bf16[16,128,256]{2,1,0:T(8,128)(2,1)} %bitcast.77), calls=%async_computation.3 | async-start | bytes 2097152 | tf_op jit(solution)/shard_map/all_to_all | solution.py:323
  157.4 159.1 %reduce-scatter.2.cloned.1.call-start = ((), (), s32[]{:S(2)}) async-start(), calls=%async_computation.6 | async-start | bytes 4456448 | tf_op jit(solution)/shard_map/reduce_scatter | solution.py:154
  157.4 1.2 copy-start.2
  158.7 1.2 copy-start.3
  202.8 1.0 copy-start.5
  211.4 2.0 collective-permute-start.1
  273.7 3.8 %collective-permute-start.2 = (f32[128,128]{1,0:T(8,128)S(1)}, f32[128,128]{1,0:T(8,128)S(1)}, u32[]{:S(2)}, u32[]{:S(2)}) collective-permute-start(f32[128,128]{1,0:T(8,128)S(1)} %convert_reduce_fusion), channel_id=1, source_target_pairs={{0,1},{1,0},{2,3},{3,2},{4,5},{5,4},{6,7},{7,6},{8,9},{9,8},{10,11... | collective-permute-start | bytes 196616 | tf_op jit(solution)/shard_map/ppermute | solution.py:335
  274.0 1.6 copy-start.7
  274.0 1.9 copy-start.10
Sparse Core Ops, SparseCore 0:
  30.8 104.7 all-gather.2
  203.0 113.4 reduce-scatter.1

commit v3 on v2

--- a/solution.py
+++ b/solution.py
@@ -141,9 +141,8 @@
     )(place.reshape(1).astype(jnp.int32), queries, kv_all, attn_cotangent)
 
 
-def gather_pair(key_states, value_states):
-    tok_rows, kv_cols = key_states.shape
-    kv = jnp.stack([key_states, value_states])
+def gather_pair(kv):
+    _, tok_rows, kv_cols = kv.shape
     return lax.all_gather(kv, "ctx", axis=0).reshape(
         lax.axis_size("ctx"), 2, 2, tok_rows // 2, kv_cols
     )
@@ -277,7 +276,7 @@
         scratch_shapes=[pltpu.VMEM((states, cols), jnp.float32)],
         compiler_params=pltpu.CompilerParams(vmem_limit_bytes=VMEM_BYTES),
         cost_estimate=pl.CostEstimate(
-            flops=8 * 10**9, bytes_accessed=8 * 1024 * 1024, transcendentals=10**6
+            flops=10**9, bytes_accessed=6 * 1024 * 1024, transcendentals=5 * 10**5
         ),
         name="scan_forward",
     )(x, b, c, col, row)
@@ -307,7 +306,7 @@
         scratch_shapes=[pltpu.VMEM((states, cols), jnp.float32)],
         compiler_params=pltpu.CompilerParams(vmem_limit_bytes=VMEM_BYTES),
         cost_estimate=pl.CostEstimate(
-            flops=16 * 10**9, bytes_accessed=12 * 1024 * 1024, transcendentals=2 * 10**6
+            flops=2 * 10**9, bytes_accessed=6 * 1024 * 1024, transcendentals=10**6
         ),
         name="scan_backward",
     )(x, dm, b, c, col, row, state)
@@ -348,16 +347,18 @@
     states = state_write.shape[1]
     folded = (count, 2, half_rows)
     share_maps = lax.axis_size("tp") == 2
-    kv_all = gather_pair(key_states, value_states)
+    kv = jnp.stack([key_states, value_states])
+    kv, sent_input, log_decay = lax.optimization_barrier((kv, ssm_input, log_decay))
+    kv_all = gather_pair(kv)
     if share_maps:
         first = lax.axis_index("tp") == 0
-        arrived = to_channels(ssm_input, jnp.where(first, state_write, state_read))
+        arrived = to_channels(sent_input, jnp.where(first, state_write, state_read))
         own_map = arrived[:, :, own_cols:]
         other_map = from_other_core(own_map)
         b_all = jnp.where(first, own_map, other_map).reshape(*folded, states)
         c_all = jnp.where(first, other_map, own_map).reshape(*folded, states)
     else:
-        arrived = to_channels(ssm_input, jnp.concatenate([state_write, state_read], axis=1))
+        arrived = to_channels(sent_input, jnp.concatenate([state_write, state_read], axis=1))
         b_all = arrived[:, :, own_cols : own_cols + states].reshape(*folded, states)
         c_all = arrived[:, :, own_cols + states :].reshape(*folded, states)
     x_all = arrived[:, :, :own_cols].reshape(*folded, own_cols)
@@ -369,8 +370,15 @@
     col = log_total.reshape(-1, 1)
     row = log_total[:, None, :]
     mixed_all, state_all = scan_forward(x_all, b_all, c_all, col, row)
+    mixed_all, kv_all = lax.optimization_barrier((mixed_all, kv_all))
+    attn_output, query_grad, dkv = attention_core(
+        queries, kv_all, attn_cotangent, lax.axis_index("ctx")
+    )
+    mixed_back = to_owners(mixed_all.reshape(count, tok_rows, own_cols))
+    dkv, mixed_back = lax.optimization_barrier((dkv, mixed_back))
+    key_grad, value_grad = scatter_pair(dkv)
     skip = jnp.repeat(skip_gain, head_dim)[None, :]
-    mixed = side_by_side(to_owners(mixed_all.reshape(count, tok_rows, own_cols)))
+    mixed = side_by_side(mixed_back)
     mixed = mixed.astype(jnp.float32) + skip * ssm_input.astype(jnp.float32)
     gate = ssm_gate.astype(jnp.float32)
     sigmoid = jax.nn.sigmoid(gate)
@@ -386,13 +394,7 @@
     d_gated = (d_normed - normed * inner_mean) / root_mean
     d_mixed = d_gated * gate * sigmoid
     gate_grad = (d_gated * mixed * sigmoid * (1.0 + gate * (1.0 - sigmoid))).astype(jnp.bfloat16)
-    d_mixed_short, kv_all = lax.optimization_barrier((d_mixed.astype(jnp.bfloat16), kv_all))
-    attn_output, query_grad, dkv = attention_core(
-        queries, kv_all, attn_cotangent, lax.axis_index("ctx")
-    )
-    dm_all = to_channels(d_mixed_short).reshape(*folded, own_cols)
-    dkv, dm_all = lax.optimization_barrier((dkv, dm_all))
-    key_grad, value_grad = scatter_pair(dkv)
+    dm_all = to_channels(d_mixed.astype(jnp.bfloat16)).reshape(*folded, own_cols)
     input_all, write_all, read_all = scan_backward(
         x_all, dm_all, b_all, c_all, col, row, state_all
     )

time: 326 us -> 297 us (0.911)
  waiting for transfers between devices: 121 us -> 77.7 us
  blocking collectives: 62.4 us -> 103 us
  starting transfers between devices: 36.9 us -> 16.7 us
  local copies, waits for them, and re-layouts: 19.3 us -> 11.9 us
    all_to_all x0 -> x1, blocking collectives: none -> 42.5 us  [to_channels(): return lax.all_to_all(blocks, 'ctx', split_axis=0, concat_axis=0)]
    all_to_all x2, waiting for transfers between devices: 43.6 us -> 4.35 us  [to_owners(): return lax.all_to_all(blocks, 'ctx', split_axis=0, concat_axis=0)]
    reduce_scatter x1, waiting for transfers between devices: 38.3 us -> 0.01 us  [scatter_pair(): lax.psum_scatter(dkv.reshape(count, 2, 2 * half_rows, kv_cols), 'ctx', sc...]
    all_gather x1, waiting for transfers between devices: 0.01 us -> 28.4 us  [gather_pair(): lax.all_gather(kv, 'ctx', axis=0)]
    all_to_all x2 -> x1, starting transfers between devices: 16.3 us -> 3.71 us  [to_channels(): return lax.all_to_all(blocks, 'ctx', split_axis=0, concat_axis=0)]
    all_to_all x2, starting transfers between devices: 20.3 us -> 12.7 us  [to_owners(): return lax.all_to_all(blocks, 'ctx', split_axis=0, concat_axis=0)]
    all_to_all x2 -> x1, waiting for transfers between devices: 36.8 us -> 43 us  [to_channels(): return lax.all_to_all(blocks, 'ctx', split_axis=0, concat_axis=0)]
    unnamed x42 -> x32, local copies, waits for them, and re-layouts: 11 us -> 5.75 us
  transfers between devices with their start and end apart: 9 -> 8, of which waited for: 5 -> 4; matrix products, arithmetic and copies ran while one was open for 6% -> 7% of each run, Pallas kernels for 17% -> 19%
where the time goes in v3:
time: 297 us; the launch traced here: 296 us
  blocking collectives  103 us (35%)
  waiting for transfers between devices  77.7 us (26%)
  Pallas kernels  55 us (19%)
  other arithmetic  17.3 us (6%)
  starting transfers between devices  16.7 us (6%)
  between operations  14.4 us (5%)
  local copies, waits for them, and re-layouts  11.9 us (4%)
    all_to_all x1, blocking collectives, to_owners(): return lax.all_to_all(blocks, 'ctx', split_axis=0, concat_axis=0)  57.6 us
    all_to_all x1, waiting for transfers between devices, to_channels(): return lax.all_to_all(blocks, 'ctx', split_axis=0, concat_axis=0)  43 us
    pallas_call x1, Pallas kernels, attention_core(): pl.pallas_call(attention_kernel, out_shape=(like_q, like_q, jax.ShapeDtyp...  42.9 us
    all_to_all x1, blocking collectives, to_channels(): return lax.all_to_all(blocks, 'ctx', split_axis=0, concat_axis=0)  42.5 us
    all_gather x1, waiting for transfers between devices, gather_pair(): lax.all_gather(kv, 'ctx', axis=0)  28.4 us
    all_to_all x2, starting transfers between devices, to_owners(): return lax.all_to_all(blocks, 'ctx', split_axis=0, concat_axis=0)  12.7 us
    pallas_call x1, Pallas kernels, scan_backward(): pl.pallas_call(functools.partial(backward_kernel, steps), grid=(steps,),...  7.37 us
  transfers between devices with their start and end apart: 8, of which 4 were waited for; matrix products, arithmetic and copies ran while one was open for 7% of the time, Pallas kernels for 19%

profile of v3, /device:TPU:0, one launch (start us, length us, event | category | flops | bytes accessed | tf_op | source)
XLA Modules:
  0.0 295.9 jit_solution(9116907774362499932)
XLA Ops:
  7.3 1.7 pad_maximum_fusion.1
  9.0 8.3 %all-to-all-start.1 = ((f32[16,1,128]{2,1,0:T(1,128)}), f32[16,1,128]{2,1,0:T(1,128)S(1)}, u32[]{:S(2)}, u32[]{:S(2)}) async-start(f32[16,1,128]{2,1,0:T(1,128)} %bitcast.89), calls=%async_computation.1 | async-start | bytes 16384 | tf_op jit(solution)/shard_map/all_to_all | solution.py:326
  17.3 1.3 copy.51
  18.8 1.4 maximum_bitcast_fusion
  20.2 4.3 %all-to-all-done.1 = f32[16,1,128]{2,1,0:T(1,128)S(1)} async-done(((f32[16,1,128]{2,1,0:T(1,128)}), f32[16,1,128]{2,1,0:T(1,128)S(1)}, u32[]{:S(2)}, u32[]{:S(2)}) %all-to-all-start.1) | async-done | bytes 8224 | tf_op jit(solution)/shard_map/all_to_all | solution.py:326
  24.5 3.7 %all-to-all-start = ((bf16[16,128,384]{2,1,0:T(8,128)(2,1)}), bf16[16,128,384]{2,1,0:T(8,128)(2,1)S(1)}, u32[]{:S(2)}, u32[]{:S(2)}) async-start(bf16[16,128,384]{2,1,0:T(8,128)(2,1)} %maximum_bitcast_fusion), calls=%async_computation | async-start | bytes 3145728 | tf_op jit(solution)/shard_map/all_to_all | solution.py:322
  28.3 0.5 broadcast.56
  28.8 0.7 reduce.3
  29.6 43.0 %all-to-all-done = bf16[16,128,384]{2,1,0:T(8,128)(2,1)S(1)} async-done(((bf16[16,128,384]{2,1,0:T(8,128)(2,1)}), bf16[16,128,384]{2,1,0:T(8,128)(2,1)S(1)}, u32[]{:S(2)}, u32[]{:S(2)}) %all-to-all-start) | async-done | bytes 1572896 | tf_op jit(solution)/shard_map/all_to_all | solution.py:322
  72.9 0.9 copy-done.9
  74.5 1.7 slice.42
  76.2 1.3 broadcast_select_fusion.2
  77.5 4.7 %scan_forward.1 = (bf16[16,2,64,256]{3,2,1,0:T(8,128)(2,1)}, bf16[8,128,256]{2,1,0:T(8,128)(2,1)S(1)}) custom-call(bf16[16,2,64,256]{3,2,1,0:T(8,128)(2,1)S(1)} %bitcast.64, bf16[16,2,64,128]{3,2,1,0:T(8,128)(2,1)S(1)} %bitcast.69, bf16[16,2,64,128]{3,2,1,0:T(8,128)(2,1)S(1)} %bitcast.67, f32[2048,1]{1,0:T(8,128)S(1)} %bitcast.62, ...), custom_call_target="tpu_custom_call" | custom-call | flops 1000000000 | bytes 6291456 | tf_op jit(solution)/shard_map/scan_forward/pallas_call | solution.py:267
  82.2 0.8 copy-done.4
  83.0 28.4 %all-gather.3.cloned.1.call-done = bf16[32,128,512]{2,1,0:T(8,128)(2,1)} async-done(((bf16[2,128,512]{2,1,0:T(8,128)(2,1)}), bf16[32,128,512]{2,1,0:T(8,128)(2,1)}) %all-gather.3.cloned.1.call-update) | async-done | bytes 4194320 | tf_op jit(solution)/shard_map/all_gather | solution.py:146
  111.4 4.3 %all-to-all-start.2 = ((bf16[16,128,256]{2,1,0:T(8,128)(2,1)}), bf16[16,128,256]{2,1,0:T(8,128)(2,1)}, u32[]{:S(2)}, u32[]{:S(2)}) async-start(bf16[16,128,256]{2,1,0:T(8,128)(2,1)} %bitcast.12), calls=%async_computation.2 | async-start | bytes 2097152 | tf_op jit(solution)/shard_map/all_to_all | solution.py:326
  115.9 1.2 copy-done.3
  117.1 42.9 %attention_both.1 = (bf16[128,4096]{1,0:T(8,128)(2,1)}, bf16[128,4096]{1,0:T(8,128)(2,1)}, bf16[16,2,2,64,512]{4,3,2,1,0:T(8,128)(2,1)}) custom-call(s32[1]{0:T(128)} %bitcast.place_ref, bf16[128,4096]{1,0:T(8,128)(2,1)S(1)} %copy-done.2, bf16[16,2,2,64,512]{4,3,2,1,0:T(8,128)(2,1)} %bitcast.92, bf16[128,4096]{1,0:T(8,128)(2,1)S(1)} %copy-done.3), custom_call_target="tpu_custom_call" | custom-call | flops 22548578304 | bytes 16777216 | tf_op jit(solution)/shard_map/attention_both/pallas_call | solution.py:117
  160.0 1.4 convert_bitcast_fusion.1
  161.8 1.0 copy-done.7
  162.8 1.0 copy-done.8
  164.1 2.4 multiply_reduce_fusion.1
  166.6 2.5 psum.7
  169.0 4.6 %fusion.7 = (bf16[128,4096]{1,0:T(8,128)(2,1)}, f32[128,4096]{1,0:T(8,128)S(1)}, bf16[128,4096]{1,0:T(8,128)(2,1)}) fusion(bf16[128,4096]{1,0:T(8,128)(2,1)S(1)} %copy-done.7, f32[128,4096]{1,0:T(8,128)} %bitcast.72, bf16[128,4096]{1,0:T(8,128)(2,1)} %param.12, f32[4096]{0:T(1024)S(1)} %bitcast.81, f32[128]{0:T(128)S(1)} %get-tuple-element.55, ...), kind=kLoop, calls=%fused_computation.11 | loop fusion | flops 11534336 | bytes 11568128 | tf_op jit(solution)/shard_map/convert_element_type | solution.py:396
  173.6 0.8 fusion.16
  174.5 42.5 %all_to_all.25 = bf16[16,128,256]{2,1,0:T(8,128)(2,1)S(1)} all-to-all(bf16[16,128,256]{2,1,0:T(8,128)(2,1)S(1)} %bitcast.77), channel_id=1, replica_groups=mesh['ctx'=16,'tp'=2] {'ctx'}, dimensions={0} | all-to-all | bytes 2097152 | tf_op jit(solution)/shard_map/all_to_all | solution.py:322
  217.0 7.4 %scan_backward.1 = (bf16[16,2,64,256]{3,2,1,0:T(8,128)(2,1)S(1)}, bf16[16,2,64,128]{3,2,1,0:T(8,128)(2,1)S(1)}, bf16[16,2,64,128]{3,2,1,0:T(8,128)(2,1)S(1)}) custom-call(bf16[16,2,64,256]{3,2,1,0:T(8,128)(2,1)S(1)} %bitcast.65, bf16[16,2,64,256]{3,2,1,0:T(8,128)(2,1)S(1)} %bitcast.66, bf16[16,2,64,128]{3,2,1,0:T(8,128)(2,1)S(1)} %bitcast.70, ...), custom_call_target="tpu_custom_call" | custom-call | flops 2000000000 | bytes 6291456 | tf_op jit(solution)/shard_map/scan_backward/pallas_call | solution.py:292
  224.6 1.9 collective-permute-done.1
  226.9 57.6 %all_to_all.26 = bf16[16,128,384]{2,1,0:T(8,128)(2,1)S(1)} all-to-all(bf16[16,128,384]{2,1,0:T(8,128)(2,1)S(1)} %pad_maximum_fusion), channel_id=1, replica_groups=mesh['ctx'=16,'tp'=2] {'ctx'}, dimensions={0} | all-to-all | bytes 3145728 | tf_op jit(solution)/shard_map/all_to_all | solution.py:326
  285.1 1.7 add_convert_fusion
  286.7 0.7 broadcast_select_fusion.4
  287.4 1.7 slice_bitcast_fusion
  (59 shorter events, 3.2 us)
Async XLA Ops:
  7.2 21.1 %copy-start = (f32[16]{0:T(128)S(1)}, f32[16]{0:T(128)}, u32[]{:S(2)}) copy-start(f32[16]{0:T(128)} %param.17) | copy-start | bytes 196
  7.2 11.5 %copy-start.13 = (bf16[128,128]{1,0:T(8,128)(2,1)S(1)}, bf16[128,128]{1,0:T(8,128)(2,1)}, u32[]{:S(2)}) copy-start(bf16[128,128]{1,0:T(8,128)(2,1)} %param.15) | copy-start | bytes 98308
  7.2 11.5 %copy-start.12 = (bf16[128,128]{1,0:T(8,128)(2,1)S(1)}, bf16[128,128]{1,0:T(8,128)(2,1)}, u32[]{:S(2)}) copy-start(bf16[128,128]{1,0:T(8,128)(2,1)} %param.14) | copy-start | bytes 98308
  7.2 104.2 %all-gather.3.cloned.1.call-start = ((), (), s32[]{:S(2)}) async-start(), calls=%async_computation.7 | async-start | bytes 4456448 | tf_op jit(solution)/shard_map/all_gather | solution.py:146
  9.0 15.5 %all-to-all-start.1 = ((f32[16,1,128]{2,1,0:T(1,128)}), f32[16,1,128]{2,1,0:T(1,128)S(1)}, u32[]{:S(2)}, u32[]{:S(2)}) async-start(f32[16,1,128]{2,1,0:T(1,128)} %bitcast.89), calls=%async_computation.1 | async-start | bytes 16384 | tf_op jit(solution)/shard_map/all_to_all | solution.py:326
  24.5 48.1 %all-to-all-start = ((bf16[16,128,384]{2,1,0:T(8,128)(2,1)}), bf16[16,128,384]{2,1,0:T(8,128)(2,1)S(1)}, u32[]{:S(2)}, u32[]{:S(2)}) async-start(bf16[16,128,384]{2,1,0:T(8,128)(2,1)} %maximum_bitcast_fusion), calls=%async_computation | async-start | bytes 3145728 | tf_op jit(solution)/shard_map/all_to_all | solution.py:322
  72.6 1.2 copy-start.9
  72.7 3.5 %collective-permute-start = (bf16[16,128,128]{2,1,0:T(8,128)(2,1)S(1)}, bf16[16,128,128]{2,1,0:T(8,128)(2,1)}, u32[]{:S(2)}, u32[]{:S(2)}) collective-permute-start(bf16[16,128,128]{2,1,0:T(8,128)(2,1)S(1)} %slice.43), channel_id=1, source_target_pairs={{0,1},{1,0},{2,3},{3,2},{4,5},{5,4},{6,7},{7,6},{8,9},{9,8},{10,11... | collective-permute-start | bytes 1572872 | tf_op jit(solution)/shard_map/ppermute | solution.py:334
  74.5 3.0 %copy-start.1 = (f32[1,2048]{0,1:T(8,128)}, f32[1,2048]{0,1:T(8,128)S(1)}, u32[]{:S(2)}) copy-start(f32[1,2048]{0,1:T(8,128)S(1)} %copy.46) | copy-start | bytes 24580
  82.2 0.8 copy-start.4
  83.0 32.9 %copy-start.2 = (bf16[128,4096]{1,0:T(8,128)(2,1)S(1)}, bf16[128,4096]{1,0:T(8,128)(2,1)}, u32[]{:S(2)}) copy-start(bf16[128,4096]{1,0:T(8,128)(2,1)} %q_ref.1) | copy-start | bytes 3145732
  111.4 48.6 %all-to-all-start.2 = ((bf16[16,128,256]{2,1,0:T(8,128)(2,1)}), bf16[16,128,256]{2,1,0:T(8,128)(2,1)}, u32[]{:S(2)}, u32[]{:S(2)}) async-start(bf16[16,128,256]{2,1,0:T(8,128)(2,1)} %bitcast.12), calls=%async_computation.2 | async-start | bytes 2097152 | tf_op jit(solution)/shard_map/all_to_all | solution.py:326
  115.8 171.6 %reduce-scatter.2.cloned.1.call-start = ((), (), s32[]{:S(2)}) async-start(), calls=%async_computation.6 | async-start | bytes 4456448 | tf_op jit(solution)/shard_map/reduce_scatter | solution.py:153
  115.9 1.2 copy-start.3
  161.5 1.3 copy-start.7
  161.5 2.3 copy-start.8
  161.5 2.6 copy-start.10
  161.5 2.6 copy-start.11
  161.8 4.8 %copy-start.6 = (f32[16,16,8,256]{3,2,0,1:T(8,128)}, f32[16,16,8,256]{3,2,0,1:T(8,128)S(1)}, u32[]{:S(2)}) copy-start(f32[16,16,8,256]{3,2,0,1:T(8,128)S(1)} %copy.43) | copy-start | bytes 6291460
  174.4 42.6 %copy-start.5 = (bf16[8,128,256]{2,1,0:T(8,128)(2,1)S(1)}, bf16[8,128,256]{2,1,0:T(8,128)(2,1)}, u32[]{:S(2)}) copy-start(bf16[8,128,256]{2,1,0:T(8,128)(2,1)} %copy-done.4) | copy-start | bytes 1572868
  224.5 2.0 collective-permute-start.1
  284.5 2.2 collective-permute-start.2
Sparse Core Ops, SparseCore 0:
  11.4 100.0 all-gather.2
  160.2 124.5 reduce-scatter.1
